TPU v7x, 128 devices: a whole 4x4x4 slice. The times are simulated.
128 devices in a mesh: grp: 4 (over y), cand: 32 (over x, z, core).
Axes of the slice: x: 4, y: 4, z: 4, core: 2. Of those that a mesh axis runs over, the one named last changes fastest.
Arguments:
- node_emb: bfloat16 [32, 512, 512], P('cand'), may hold values from -6 to 6
- rel_emb: float32 [900, 512], P('grp'), may hold values from -6 to 6
- w_in: bfloat16 [512, 512], replicated, may hold values from -0.25 to 0.25
- w_self: bfloat16 [512, 512], replicated, may hold values from -1 to 1
- rel_score: float32 [900, 512], replicated, may hold values from -7 to 7
- mirror_blocks: int32 [4, 32, 32, 1], P('grp', 'cand'), may hold values from 0 to 3
- adj_values: bfloat16 [4, 32, 192, 128, 128], P('grp', 'cand'), may hold values from -0.0390625 to 0.0390625
- adj_source: int32 [4, 32, 192], P('grp', 'cand'), may hold values from 0 to 31
- adj_target: int32 [4, 32, 192], P('grp', 'cand'), may hold values from 0 to 3
- adj_relation: int32 [4, 32, 192], P('grp', 'cand'), may hold values from 0 to 224
- live_blocks: int32 [4, 32], P('grp', 'cand'), may hold values from 48 to 192, as said below
- query_head: int32 [1024], replicated, may hold values from 0 to 16383
- query_rel: int32 [1024], replicated, may hold values from 0 to 899
- allowed: int32 [1024, 8], replicated, may hold values from 0 to 127, as said below
- true_tail: int32 [1024], replicated, may hold values from 0 to 16383, as said below
Outputs:
- h_out: bfloat16 [32, 512, 512], P('cand', 'grp')
- loss: float32 [1024], replicated
- grad_h: float32 [32, 512, 512], P('cand', 'grp')
- grad_rel: float32 [900, 512], P('grp')
- grad_w_in: float32 [512, 512], replicated
- grad_w_self: float32 [512, 512], replicated
Inputs may be any that keep to these rules, and one draw needn't show every extreme that they name: `live_blocks`: blocks from this count on are padding; on some device all 192 blocks are live. `allowed`: ids of blocks of 128 concepts; a query may name a block twice. `true_tail`: lies in one of the query's allowed blocks.
All inputs are finite; a program needn't handle non-finite values.
Results may differ from a plain program's by a relative error of at most 0.011.
Values may be sent and summed in bfloat16 or wider, within the bound.
A program may use at most 128 MiB of HBM per device.

v0:
```python
import math

import jax
import jax.numpy as jnp
from jax import lax
from jax.sharding import PartitionSpec as P

NEG_FILL = -1e30
HIGH = lax.Precision.HIGHEST


def body(
    node_emb,
    rel_emb,
    w_in,
    w_self,
    rel_score,
    mirror_blocks,
    adj_values,
    adj_source,
    adj_target,
    adj_relation,
    live_blocks,
    query_head,
    query_rel,
    allowed,
    true_tail,
):
    cand_count = lax.axis_size("cand")
    grp_count = lax.axis_size("grp")
    grp_index = lax.axis_index("grp")
    cand_index = lax.axis_index("cand")
    nodes = node_emb[0]
    node_rows, feature_dim = nodes.shape
    block_rows = adj_values.shape[-1]
    tile_count = node_rows // block_rows
    share_rows = node_rows // grp_count
    wanted = mirror_blocks[0, 0]
    slot_count = wanted.shape[1]
    mirror_count = cand_count * slot_count
    requested = lax.all_to_all(wanted, "cand", split_axis=0, concat_axis=0, tiled=True)
    everything = lax.all_gather(node_emb, "cand", axis=0, tiled=True)
    everything = everything.reshape(cand_count * tile_count, block_rows, feature_dim)
    owners = jnp.arange(cand_count, dtype=jnp.int32)[:, None] * tile_count
    mirrors = jnp.take(everything, (owners + wanted).reshape(-1), axis=0)
    tile_values = adj_values[0, 0]
    block_count = tile_values.shape[0]
    stride = math.gcd(block_count, 16)
    turns = block_count // stride
    live_mask = (jnp.arange(block_count, dtype=jnp.int32) < live_blocks[0, 0]).astype(jnp.float32)
    packed = (
        tile_values.reshape(turns, stride, block_rows, block_rows),
        adj_source[0, 0].reshape(turns, stride),
        adj_target[0, 0].reshape(turns, stride),
        adj_relation[0, 0].reshape(turns, stride),
        live_mask.reshape(turns, stride),
    )

    def forward_turn(partial_value, inputs_now):
        values_now, source_now, target_now, relation_now, live_now = inputs_now
        composed = (
            jnp.take(mirrors, source_now, axis=0).astype(jnp.float32)
            - jnp.take(rel_emb, relation_now, axis=0)[:, None, :]
        ).astype(jnp.bfloat16)
        messages = jnp.einsum(
            "bij,bjd->bid", values_now, composed, preferred_element_type=jnp.float32
        )
        messages = messages * live_now[:, None, None]
        return (partial_value.at[target_now].add(messages), None)

    partial_value, ignored = lax.scan(
        forward_turn, jnp.zeros((tile_count, block_rows, feature_dim), jnp.float32), packed
    )
    aggregate = lax.psum_scatter(
        partial_value.reshape(node_rows, feature_dim), "grp", scatter_dimension=0, tiled=True
    )
    aggregate_bf = aggregate.astype(jnp.bfloat16)
    own_rows = lax.dynamic_slice_in_dim(nodes, grp_index * share_rows, share_rows, 0)
    pre_act = jnp.dot(aggregate_bf, w_in, preferred_element_type=jnp.float32) + jnp.dot(
        own_rows, w_self, preferred_element_type=jnp.float32
    )
    activated = jnp.tanh(pre_act)
    h_new = activated.astype(jnp.bfloat16)
    first_row = cand_index * node_rows + grp_index * share_rows
    row_ids = first_row + jnp.arange(share_rows, dtype=jnp.int32)
    head_pick = query_head[:, None] == row_ids[None, :]
    head_part = jnp.dot(head_pick.astype(jnp.bfloat16), h_new, preferred_element_type=jnp.float32)
    heads = lax.psum(head_part, ("grp", "cand"))
    queries = heads + jnp.take(rel_score, query_rel, axis=0)
    cand_rows = h_new.astype(jnp.float32)
    scale = feature_dim ** (-0.5)
    cross = jnp.dot(queries, cand_rows.T, precision=HIGH)
    scores = -scale * (
        jnp.sum(queries * queries, axis=1)[:, None]
        + jnp.sum(cand_rows * cand_rows, axis=1)[None, :]
        - 2.0 * cross
    )
    block_ids = first_row // block_rows + jnp.arange(share_rows // block_rows, dtype=jnp.int32)
    block_ok = jnp.any(allowed[:, :, None] == block_ids[None, None, :], axis=1)
    allowed_mask = jnp.repeat(block_ok, block_rows, axis=1)
    tail_pick = true_tail[:, None] == row_ids[None, :]
    truth_part = jnp.sum(jnp.where(tail_pick, scores, 0.0), axis=1)
    local_max = jnp.max(jnp.where(allowed_mask, scores, NEG_FILL), axis=1)
    row_max = lax.pmax(local_max, ("grp", "cand"))
    local_total = jnp.sum(
        jnp.exp(jnp.where(allowed_mask, scores - row_max[:, None], NEG_FILL)), axis=1
    )
    row_total, truth = lax.psum((local_total, truth_part), ("grp", "cand"))
    log_norm = row_max + jnp.log(row_total)
    loss = log_norm - truth
    prob = jnp.exp(jnp.where(allowed_mask, scores - log_norm[:, None], NEG_FILL))
    grad_score = (prob - tail_pick.astype(jnp.float32)) / query_head.shape[0]
    query_part = (
        2.0
        * scale
        * (
            jnp.dot(grad_score, cand_rows, precision=HIGH)
            - queries * jnp.sum(grad_score, axis=1)[:, None]
        )
    )
    query_grad = lax.psum(query_part, ("grp", "cand"))
    cand_grad = (
        2.0
        * scale
        * (
            jnp.dot(grad_score.T, queries, precision=HIGH)
            - cand_rows * jnp.sum(grad_score, axis=0)[:, None]
        )
    )
    row_grad = cand_grad + jnp.dot(head_pick.astype(jnp.float32).T, query_grad, precision=HIGH)
    pre_grad = (row_grad * (1.0 - activated * activated)).astype(jnp.bfloat16)
    grad_w_in, grad_w_self = lax.psum(
        (
            jnp.dot(aggregate_bf.T, pre_grad, preferred_element_type=jnp.float32),
            jnp.dot(own_rows.T, pre_grad, preferred_element_type=jnp.float32),
        ),
        ("grp", "cand"),
    )
    agg_grad = jnp.dot(pre_grad, w_in.T, preferred_element_type=jnp.float32).astype(jnp.bfloat16)
    agg_tiles = lax.all_gather(agg_grad, "grp", axis=0, tiled=True).reshape(
        tile_count, block_rows, feature_dim
    )

    def backward_turn(carry, inputs_now):
        mirror_grad, relation_grad = carry
        values_now, source_now, target_now, relation_now, live_now = inputs_now
        composed_grad = jnp.einsum(
            "bij,bid->bjd",
            values_now,
            jnp.take(agg_tiles, target_now, axis=0),
            preferred_element_type=jnp.float32,
        )
        composed_grad = composed_grad * live_now[:, None, None]
        mirror_grad = mirror_grad.at[source_now].add(composed_grad)
        relation_grad = relation_grad.at[relation_now].add(-jnp.sum(composed_grad, axis=1))
        return ((mirror_grad, relation_grad), None)

    start = (
        jnp.zeros((mirror_count, block_rows, feature_dim), jnp.float32),
        jnp.zeros(rel_emb.shape, jnp.float32),
    )
    (mirror_grad, relation_grad), ignored = lax.scan(backward_turn, start, packed)
    grad_rel = lax.psum(relation_grad, "cand")
    returned = lax.all_to_all(
        mirror_grad.reshape(cand_count, slot_count, block_rows, feature_dim).astype(jnp.bfloat16),
        "cand",
        split_axis=0,
        concat_axis=0,
        tiled=True,
    ).astype(jnp.float32)
    owned = (
        jnp.zeros((tile_count, block_rows, feature_dim), jnp.float32)
        .at[requested.reshape(-1)]
        .add(returned.reshape(mirror_count, block_rows, feature_dim))
    )
    node_grad = lax.psum_scatter(
        owned.reshape(node_rows, feature_dim).astype(jnp.bfloat16),
        "grp",
        scatter_dimension=0,
        tiled=True,
    ).astype(jnp.float32)
    node_grad = node_grad + jnp.dot(pre_grad, w_self.T, preferred_element_type=jnp.float32)
    return (h_new[None], loss, node_grad[None], grad_rel, grad_w_in, grad_w_self)


def solution(mesh):
    return jax.shard_map(
        body,
        mesh=mesh,
        in_specs=(
            P("cand", None, None),
            P("grp", None),
            P(),
            P(),
            P(),
            P("grp", "cand", None, None),
            P("grp", "cand", None, None, None),
            P("grp", "cand", None),
            P("grp", "cand", None),
            P("grp", "cand", None),
            P("grp", "cand"),
            P(),
            P(),
            P(),
            P(),
        ),
        out_specs=(P("cand", "grp", None), P(), P("cand", "grp", None), P("grp", None), P(), P()),
        check_vma=False,
    )
```

profile of v0, /device:TPU:1, one launch (start us, length us, event | category | flops | bytes accessed | tf_op | source)
XLA Modules:
  0.0 1358.6 jit_solution(7435921861001893714)
XLA Ops:
  14.8 71.8 %all-gather.2.cloned.1.call-done = bf16[32,512,512]{2,1,0:T(8,128)(2,1)} async-done(((bf16[1,512,512]{2,1,0:T(8,128)(2,1)}), bf16[32,512,512]{2,1,0:T(8,128)(2,1)}) %all-gather.2.cloned.1.call-update) | async-done | bytes 16777232 | tf_op jit(solution)/shard_map/all_gather | solution.py:42
  86.6 8.5 gather_fusion.3
  95.1 4.6 broadcast_select_fusion.1
  99.8 187.6 %while.22 = (s32[]{:T(128)}, f32[4,128,512]{2,1,0:T(8,128)S(1)}, s32[12,16]{1,0:T(8,128)S(1)}, bf16[12,16,128,128]{3,2,1,0:T(8,128)(2,1)}, s32[12,16]{1,0:T(8,12...) while((s32[]{:T(128)}, f32[4,128,512]{2,1,0:T(8,128)S(1)}, ...), condition=%wide.region_2.3_spmd, body=%wide.region_0.0_spmd.sunk | while | flops 274737504 | bytes 23766708 | solution.py:71
  104.8 4.6 convolution_multiply_fusion.4
  109.4 6.1 scatter_fusion
  120.4 4.6 convolution_multiply_fusion.4
  125.0 6.1 scatter_fusion
  136.0 4.6 convolution_multiply_fusion.4
  140.6 6.1 scatter_fusion
  151.7 4.6 convolution_multiply_fusion.4
  156.2 6.1 scatter_fusion
  167.3 4.6 convolution_multiply_fusion.4
  171.8 6.1 scatter_fusion
  182.9 4.6 convolution_multiply_fusion.4
  187.5 6.1 scatter_fusion
  198.5 4.6 convolution_multiply_fusion.4
  203.1 6.1 scatter_fusion
  214.2 4.6 convolution_multiply_fusion.4
  218.7 6.1 scatter_fusion
  229.8 4.6 convolution_multiply_fusion.4
  234.4 6.1 scatter_fusion
  245.4 4.6 convolution_multiply_fusion.4
  250.0 6.1 scatter_fusion
  261.1 4.6 convolution_multiply_fusion.4
  265.7 6.1 scatter_fusion
  276.7 4.6 convolution_multiply_fusion.4
  281.3 6.1 scatter_fusion
  288.5 21.3 %reduce-scatter.3.cloned.1.call-done = f32[128,512]{1,0:T(8,128)} async-done(((f32[512,512]{1,0:T(8,128)}), f32[128,512]{1,0:T(8,128)}) %reduce-scatter.3.cloned.1.call-update) | async-done | bytes 262160 | tf_op jit(solution)/shard_map/reduce_scatter | solution.py:74
  314.4 4.9 gather_fusion.4
  319.3 147.6 %all-reduce.6.cloned.1.call-done = f32[1024,512]{1,0:T(8,128)} async-done(((f32[1024,512]{1,0:T(8,128)}), f32[1024,512]{1,0:T(8,128)}) %all-reduce.6.cloned.1.call-update) | async-done | bytes 2097168 | tf_op jit(solution)/shard_map/psum | solution.py:88
  472.4 63.8 %pmax.7 = f32[1024]{0:T(1024)S(1)} all-reduce(f32[1024]{0:T(1024)S(1)} %get-tuple-element.185), channel_id=1, replica_groups=mesh['grp'=4,'cand'=32] {'grp','cand'}, use_global_device_ids=true, to_apply=%region_9.10 | all-reduce | flops 1024 | bytes 8192 | tf_op jit(solution)/shard_map/pmax | solution.py:104
  536.3 63.8 %psum.50 = f32[1024]{0:T(1024)S(1)} all-reduce(f32[1024]{0:T(1024)S(1)} %exponential_reduce_fusion), channel_id=1, replica_groups=mesh['grp'=4,'cand'=32] {'grp','cand'}, use_global_device_ids=true, to_apply=%region_11.12 | all-reduce | flops 1024 | bytes 8192 | tf_op jit(solution)/shard_map/psum | solution.py:108
  605.9 4.7 all-to-all-start
  610.7 8.6 copy.26
  622.3 130.1 %all-reduce.8.cloned.1.call-done = f32[1024,512]{1,0:T(8,128)} async-done(((f32[1024,512]{1,0:T(8,128)}), f32[1024,512]{1,0:T(8,128)}) %all-reduce.8.cloned.1.call-update) | async-done | bytes 2097168 | tf_op jit(solution)/shard_map/psum | solution.py:121
  755.2 10.5 all_gather.7
  770.0 204.1 %while.23 = (s32[]{:T(128)}, f32[32,128,512]{2,1,0:T(8,128)}, f32[225,512]{1,0:T(8,128)S(1)}, s32[12,16]{1,0:T(8,128)S(1)}, bf16[12,16,128,128]{2,3,1,0:T(8,128)...) while((s32[]{:T(128)}, f32[32,128,512]{2,1,0:T(8,128)}, ...), condition=%wide.region_21.22_spmd, body=%wide.region_17.21_spmd.sunk | while | flops 272639232 | bytes 24124884 | solution.py:162
  776.6 9.5 scatter_fusion.1
  789.1 4.5 fusion.96
  793.6 9.4 scatter_fusion.1
  805.9 4.5 fusion.96
  810.5 9.5 scatter_fusion.1
  827.4 9.5 scatter_fusion.1
  844.4 9.5 scatter_fusion.1
  856.8 4.5 fusion.96
  861.3 9.6 scatter_fusion.1
  873.9 4.5 fusion.96
  878.4 9.8 scatter_fusion.1
  891.1 4.5 fusion.96
  895.6 9.6 scatter_fusion.1
  912.7 9.3 scatter_fusion.1
  925.0 4.5 fusion.96
  929.5 9.8 scatter_fusion.1
  946.8 9.4 scatter_fusion.1
  963.6 9.6 scatter_fusion.1
  974.1 6.1 convert_bitcast_fusion
  980.3 9.7 all-to-all-start.1
  990.7 51.4 %all-to-all-done.1 = bf16[32,1,128,512]{3,2,1,0:T(8,128)(2,1)} async-done(((bf16[32,1,128,512]{3,2,1,0:T(8,128)(2,1)}), bf16[32,1,128,512]{3,2,1,0:T(8,128)(2,1)}, u32[]{:S(2)}, u32[]{:S(2)}) %all-to-all-start.1) | async-done | bytes 4194336 | tf_op jit(solution)/shard_map/all_to_all | solution.py:164
  1042.1 6.6 bitcast_convert_fusion
  1048.7 11.7 scatter_fusion.2
  1065.4 65.0 %psum.51 = f32[1024]{0:T(1024)S(1)} all-reduce(f32[1024]{0:T(1024)S(1)} %get-tuple-element.133), channel_id=1, replica_groups=mesh['grp'=4,'cand'=32] {'grp','cand'}, use_global_device_ids=true, to_apply=%region_13.14 | all-reduce | flops 1024 | bytes 8192 | tf_op jit(solution)/shard_map/psum | solution.py:108
  1133.0 56.9 %all-reduce.10.cloned.1.call-done = f32[225,512]{1,0:T(8,128)} async-done(((f32[225,512]{1,0:T(8,128)}), f32[225,512]{1,0:T(8,128)}) %all-reduce.10.cloned.1.call-update) | async-done | bytes 460816 | tf_op jit(solution)/shard_map/psum | solution.py:163
  1189.9 156.6 %all-reduce.12.cloned.1.call-done = (f32[512,512]{1,0:T(8,128)}, f32[512,512]{1,0:T(8,128)}) async-done(((f32[512,512]{1,0:T(8,128)}, f32[512,512]{1,0:T(8,128)}), (f32[512,512]{1,0:T(8,128)}, f32[512,512]{1,0:T(8,128)})) %all-reduce.12.cloned.1.call-update) | async-done | bytes 2097168 | tf_op jit(solution)/shard_map/psum | solution.py:132
  (288 shorter events, 168.2 us)
Async XLA Ops:
  7.2 307.2 %copy-start = (f32[900,512]{1,0:T(8,128)S(1)}, f32[900,512]{1,0:T(8,128)}, u32[]{:S(2)}) copy-start(f32[900,512]{1,0:T(8,128)} %param.23) | copy-start | bytes 5529604
  7.2 79.4 %all-gather.2.cloned.1.call-start = ((), (), s32[]{:S(2)}) async-start(), calls=%async_computation.4 | async-start | bytes 17301504 | tf_op jit(solution)/shard_map/all_gather | solution.py:42
  7.9 301.9 %reduce-scatter.3.cloned.1.call-start = ((), (), s32[]{:S(2)}) async-start(), calls=%async_computation.5 | async-start | bytes 1310720 | tf_op jit(solution)/shard_map/reduce_scatter | solution.py:74
  95.1 4.8 copy-start.4
  287.4 1.0 copy-start.2
  287.4 23.7 %copy-start.7 = (bf16[512,512]{1,0:T(8,128)(2,1)S(1)}, bf16[512,512]{1,0:T(8,128)(2,1)}, u32[]{:S(2)}) copy-start(bf16[512,512]{1,0:T(8,128)(2,1)} %param.22) | copy-start | bytes 1572868
  287.4 24.9 %copy-start.13 = (s32[1024]{0:T(1024)S(1)}, s32[1024]{0:T(1024)}, u32[]{:S(2)}) copy-start(s32[1024]{0:T(1024)} %param.30) | copy-start | bytes 12292
  288.4 178.5 %all-reduce.6.cloned.1.call-start = ((), (), s32[]{:S(2)}) async-start(), calls=%async_computation.6 | async-start | bytes 4194304 | tf_op jit(solution)/shard_map/psum | solution.py:88
  312.4 306.9 %copy-start.5 = (bf16[128,512]{1,0:T(8,128)(2,1)}, bf16[128,512]{1,0:T(8,128)(2,1)S(1)}, u32[]{:S(2)}) copy-start(bf16[128,512]{1,0:T(8,128)(2,1)S(1)} %get-tuple-element.175) | copy-start | bytes 393220
  312.4 2.0 copy-start.14
  314.3 438.1 %all-reduce.8.cloned.1.call-start = ((), (), s32[]{:S(2)}) async-start(), calls=%async_computation.7 | async-start | bytes 4194304 | tf_op jit(solution)/shard_map/psum | solution.py:121
  314.4 4.9 copy-start.12
  469.7 1.3 copy-start.3
  469.8 130.4 %copy-start.11 = (s32[1024]{0:T(1024)S(1)}, s32[1024]{0:T(1024)}, u32[]{:S(2)}) copy-start(s32[1024]{0:T(1024)} %param.33) | copy-start | bytes 12292
  604.6 0.7 copy-start.15
  605.9 374.3 %all-to-all-start = ((s32[32,1,1]{2,1,0:T(1,128)}), s32[32,1,1]{2,1,0:T(1,128)S(1)}, u32[]{:S(2)}, u32[]{:S(2)}) async-start(s32[32,1,1]{2,1,0:T(1,128)} %copy.28), calls=%async_computation.1 | async-start | bytes 32768 | tf_op jit(solution)/shard_map/all_to_all | solution.py:41
  622.3 132.6 %copy-start.6 = (bf16[512,512]{1,0:T(8,128)(2,1)S(1)}, bf16[512,512]{1,0:T(8,128)(2,1)}, u32[]{:S(2)}) copy-start(bf16[512,512]{1,0:T(8,128)(2,1)} %param.21) | copy-start | bytes 1572868
  974.1 6.2 copy-start.8
  980.3 61.8 %all-to-all-start.1 = ((bf16[32,1,128,512]{3,2,1,0:T(8,128)(2,1)}), bf16[32,1,128,512]{3,2,1,0:T(8,128)(2,1)}, u32[]{:S(2)}, u32[]{:S(2)}) async-start(bf16[32,1,128,512]{3,2,1,0:T(8,128)(2,1)} %convert_bitcast_fusion), calls=%async_computation.2 | async-start | bytes 8388608 | tf_op jit(solution)/shard_map/all_to_all | solution.py:164
  989.9 141.1 %reduce-scatter.5.cloned.1.call-start = ((), (), s32[]{:S(2)}) async-start(), calls=%async_computation.8 | async-start | bytes 655360 | tf_op jit(solution)/shard_map/reduce_scatter | solution.py:176
  1060.4 1.5 copy-start.10
  1061.3 128.6 %all-reduce.10.cloned.1.call-start = ((), (), s32[]{:S(2)}) async-start(), calls=%async_computation.9 | async-start | bytes 950272 | tf_op jit(solution)/shard_map/psum | solution.py:163
  1061.9 284.7 %all-reduce.12.cloned.1.call-start = ((), (), s32[]{:S(2)}) async-start(), calls=%async_computation.10 | async-start | bytes 4194304 | tf_op jit(solution)/shard_map/psum | solution.py:132
  1346.6 4.2 copy-start.9
  1346.6 5.2 copy-start.1
Sparse Core Ops, SparseCore 0:
  10.3 76.2 all-gather.1
  288.5 21.1 reduce-scatter.2
  314.6 152.1 all-reduce.5
  604.7 147.5 all-reduce.7
  1061.4 18.1 reduce-scatter.4
  1083.3 106.5 all-reduce.9
  1195.5 150.9 all-reduce.11
where the time goes:
time: 1360 us
  waiting for transfers between devices  637 us (47%)
  other arithmetic  240 us (18%)
  blocking collectives  203 us (15%)
  matrix products  130 us (10%)
  local copies, waits for them, and re-layouts  117 us (9%)
  between operations  15.1 us (1%)
  starting transfers between devices  14.7 us (1%)
    psum x1, waiting for transfers between devices, body(): lax.psum((jnp.dot(aggregate_bf.T, pre_grad, preferred_element_type=jnp.fl...  157 us
    psum x1, waiting for transfers between devices, body(): heads = lax.psum(head_part, ('grp', 'cand'))  148 us
    psum x1, waiting for transfers between devices, body(): query_grad = lax.psum(query_part, ('grp', 'cand'))  130 us
    psum x2, blocking collectives, body(): row_total, truth = lax.psum((local_total, truth_part), ('grp', 'cand'))  129 us
    scatter-add x12, other arithmetic, backward_turn(): mirror_grad = mirror_grad.at[source_now].add(composed_grad)  115 us
    scatter-add x12, other arithmetic, forward_turn(): return (partial_value.at[target_now].add(messages), None)  73.3 us
    all_gather x1, waiting for transfers between devices, body(): everything = lax.all_gather(node_emb, 'cand', axis=0, tiled=True)  71.8 us
    pmax x1, blocking collectives, body(): row_max = lax.pmax(local_max, ('grp', 'cand'))  63.8 us
  transfers between devices with their start and end apart: 9, of which 7 were waited for; matrix products, arithmetic and copies ran while one was open for 18% of the time, Pallas kernels for 0%

commit v1 on v0

v1 whole, which is shorter than its diff:
```python
import functools

import jax
import jax.numpy as jnp
from jax import lax
from jax.experimental import pallas as pl
from jax.experimental.pallas import tpu as pltpu
from jax.sharding import PartitionSpec as P

NEG_FILL = -1e30
MESH = pl.DeviceIdType.MESH
BF = jnp.bfloat16
F32 = jnp.float32
NN = (((1,), (0,)), ((), ()))
NT = (((1,), (1,)), ((), ()))
TN = (((0,), (0,)), ((), ()))
VMEM_SPEC = pl.BlockSpec(memory_space=pltpu.VMEM)
SMEM_SPEC = pl.BlockSpec(memory_space=pltpu.SMEM)
ANY_SPEC = pl.BlockSpec(memory_space=pl.ANY)
LIMIT = 60 * 1024 * 1024
STAGES = (("z", "x", "y"), ("x", "z", "y"))
STAGES_CAND = (("z", "x"), ("x", "z"))


def dot(a, b, dims=NN):
    return lax.dot_general(a, b, dims, preferred_element_type=F32)


class Place:
    def __init__(self):
        self.g = lax.axis_index("grp")
        self.c = lax.axis_index("cand")
        self.x = self.c // 8
        self.zk = self.c % 8
        self.z = self.zk // 2
        self.k = self.c % 2
        self.xk = self.x * 2 + self.k

    def dev(self, g, c):
        return {"grp": g, "cand": c}

    def at(self, axis):
        return {"x": self.x, "z": self.z, "y": self.g}[axis]

    def peer(self, axis, other):
        if axis == "y":
            return self.dev(other, self.c)
        if axis == "x":
            return self.dev(self.g, other * 8 + self.zk)
        return self.dev(self.g, self.x * 8 + other * 2 + self.k)

    def sibling(self):
        return self.dev(self.g, self.c + 1 - 2 * self.k)


def enter(devices):
    barrier = pltpu.get_barrier_semaphore()
    for device in devices:
        pl.semaphore_signal(barrier, inc=1, device_id=device, device_id_type=MESH)
    pl.semaphore_wait(barrier, len(devices))


def ring_devices(me):
    found = [me.sibling()]
    for axis in ("y", "x", "z"):
        for d in (1, 2, 3):
            found.append(me.peer(axis, (me.at(axis) + d) % 4))
    return found


class Wire:
    def __init__(self, send_sem, recv_sem):
        self.send_sem, self.recv_sem, self.count, self.sent = send_sem, recv_sem, 0, []

    def put(self, src, dst, device):
        at = self.count
        self.count += 1
        copy = pltpu.make_async_remote_copy(
            src_ref=src,
            dst_ref=dst,
            send_sem=self.send_sem.at[at],
            recv_sem=self.recv_sem.at[at],
            device_id=device,
            device_id_type=MESH,
        )
        copy.start()
        self.sent.append(copy)
        return copy

    def drain(self):
        for copy in self.sent:
            copy.wait_send()


def add_up(read_terms, write, count):
    chunk = min(count, 8)

    def one(i, carry):
        at = pl.ds(i * chunk, chunk)
        terms = read_terms(at)
        total = terms[0].astype(F32)
        for term in terms[1:]:
            total = total + term.astype(F32)
        write(at, total)
        return carry

    if count == chunk:
        one(0, 0)
    else:
        lax.fori_loop(0, count // chunk, one, 0)


class AllReduce:
    @staticmethod
    def scratch(shards, stages):
        depth = len(stages[0])
        shapes = [
            pltpu.VMEM((4, shards, 16, 128), BF),
            pltpu.VMEM((2, shards, 16, 128), BF),
            pltpu.VMEM((4, shards, 16, 128), BF),
        ]
        for level in range(depth):
            shapes.append(pltpu.VMEM((2, shards // 4**level, 16, 128), BF))
            shapes.append(pltpu.VMEM((2, 3, shards // 4 ** (level + 1), 16, 128), BF))
        return shapes

    def __init__(self, me, wire, shards, stages, refs):
        self.me, self.wire, self.shards, self.stages = me, wire, shards, stages
        self.part, self.rcore, self.out = refs[:3]
        depth = len(stages[0])
        self.acc = refs[3 : 3 + 2 * depth : 2]
        self.recv = refs[4 : 4 + 2 * depth : 2]
        self.sizes = [shards // 4 ** (i + 1) for i in range(depth)]

    def steps(self):
        me, wire = self.me, self.wire
        mine = 2 * me.k
        copy = wire.put(self.part.at[pl.ds(2 - mine, 2)], self.rcore, me.sibling())
        yield
        copy.wait_recv()
        for col in range(2):

            def write(at, value, col=col):
                self.acc[0][col, at] = value.astype(BF)

            add_up(
                lambda at, col=col: (self.part[mine + col, at], self.rcore[col, at]),
                write,
                self.shards,
            )
        offsets = [0, 0]
        history = []
        depth = len(self.sizes)
        for level in range(depth):
            size = self.sizes[level]
            copies = []
            for d in (1, 3, 2):
                for col in range(2):
                    axis = self.stages[col][level]
                    other = (me.at(axis) + d) % 4
                    copies.append(
                        wire.put(
                            self.acc[level].at[col, pl.ds(other * size, size)],
                            self.recv[level].at[col, d - 1],
                            me.peer(axis, other),
                        )
                    )
            yield
            for copy in copies:
                copy.wait_recv()
            for col in range(2):
                own = me.at(self.stages[col][level]) * size
                offsets[col] = offsets[col] + own

                def terms(at, col=col, own=own, level=level):
                    base = pl.ds(own + at.start, at.size)
                    return [self.acc[level][col, base]] + [
                        self.recv[level][col, d, at] for d in range(3)
                    ]

                def write(at, value, col=col, level=level):
                    if level + 1 < depth:
                        self.acc[level + 1][col, at] = value.astype(BF)
                    else:
                        self.out[mine + col, pl.ds(offsets[col] + at.start, at.size)] = (
                            value.astype(BF)
                        )

                add_up(terms, write, size)
            history.append(tuple(offsets))
        for level in reversed(range(depth)):
            size = self.sizes[level]
            copies = []
            for d in (1, 3, 2):
                for col in range(2):
                    axis = self.stages[col][level]
                    other = (me.at(axis) + d) % 4
                    place = self.out.at[mine + col, pl.ds(history[level][col], size)]
                    copies.append(wire.put(place, place, me.peer(axis, other)))
            yield
            for copy in copies:
                copy.wait_recv()
        place = self.out.at[pl.ds(mine, 2)]
        copy = wire.put(place, place, me.sibling())
        yield
        copy.wait_recv()

    def run(self):
        for ignored in self.steps():
            pass


def run_together(*reduces):
    live = [r.steps() for r in reduces]
    while live:
        still = []
        for steps in live:
            try:
                next(steps)
                still.append(steps)
            except StopIteration:
                pass
        live = still


def fetch_kernel(
    node, wanted_v, w_self,
    mirrors, requests, self_part,
    wanted_row, request_s, staged, send_sem, recv_sem, local_sem, *gathered,
):
    me = Place()
    devices = []
    for e in range(1, 8):
        devices.append(me.dev(me.g, me.x * 8 + (me.zk + e) % 8))
    for e in range(1, 8):
        other = (me.xk + e) % 8
        if e == 7:
            pass
        devices.append(me.dev(me.g, (other // 2) * 8 + me.z * 2 + other % 2))
    enter(devices)
    wire = Wire(send_sem, recv_sem)
    wanted_row[...] = jnp.zeros_like(wanted_row)
    wanted_row[:, 0:32] = wanted_v[...]
    halves = (pl.ds(0, 256), pl.ds(256, 256))
    first = {}
    for d in (1, 3, 2):
        for col, axis in ((0, "x"), (1, "z")):
            other = (me.at(axis) + d) % 4
            first[col, d] = wire.put(
                node.at[:, :, halves[col]], gathered[3 * col + d - 1], me.peer(axis, other)
            )
    asks = []
    for e in range(1, 8):
        for col in range(2):
            asks.append(
                wire.put(
                    wanted_row,
                    requests.at[8 * col + (me.zk if col == 0 else me.xk)],
                    devices[7 * col + e - 1],
                )
            )
    requests[me.zk] = wanted_row[...]
    requests[8 + me.xk] = wanted_row[...]
    for copy in asks:
        copy.wait_recv()
    local = pltpu.make_async_copy(requests, request_s, local_sem)
    local.start()
    local.wait()
    moved = []
    for d in (0, 1, 3, 2):
        for col, axis in ((0, "x"), (1, "z")):
            if d:
                first[col, d].wait_recv()
            origin = (me.at(axis) + 4 - d) % 4
            own_slot = me.zk if col == 0 else me.xk
            owner = origin * 8 + me.zk if col == 0 else me.x * 8 + origin * 2 + me.k
            for e in range(8):
                slot = (own_slot + e) % 8
                index = request_s[8 * col + slot, 0, owner]
                if d:
                    tile = gathered[3 * col + d - 1][index]
                else:
                    tile = node[index, :, 256 * col : 256 * col + 256]
                if e == 0:
                    mirrors[col, own_slot, origin] = tile
                else:
                    staged[col, e - 1, d] = tile
                    moved.append(
                        wire.put(
                            staged.at[col, e - 1, d],
                            mirrors.at[col, own_slot, origin],
                            devices[7 * col + e - 1],
                        )
                    )

    self_part[...] = dot(node[me.g], w_self[...])
    for copy in moved:
        copy.wait_recv()
    wire.drain()


def fetch(node_tiles, wanted, w_self):
    depth = node_tiles.shape[2]
    copies = 6 + 14 + 56
    return pl.pallas_call(
        fetch_kernel,
        name="fetch",
        out_shape=(
            jax.ShapeDtypeStruct((2, 8, 4, 128, 256), BF),
            jax.ShapeDtypeStruct((16, 1, 128), jnp.int32),
            jax.ShapeDtypeStruct((128, depth), F32),
        ),
        in_specs=[VMEM_SPEC] * 3,
        out_specs=(VMEM_SPEC,) * 3,
        scratch_shapes=[
            pltpu.VMEM((1, 128), jnp.int32),
            pltpu.SMEM((16, 1, 128), jnp.int32),
            pltpu.VMEM((2, 7, 4, 128, 256), BF),
            pltpu.SemaphoreType.DMA((copies,)),
            pltpu.SemaphoreType.DMA((copies,)),
            pltpu.SemaphoreType.DMA,
            *[pltpu.VMEM((4, 128, 256), BF)] * 6,
        ],
        compiler_params=pltpu.CompilerParams(
            collective_id=0, has_side_effects=True, vmem_limit_bytes=LIMIT
        ),
    )(node_tiles, wanted, w_self)


GROUP = 8


def slots_of(source):
    x, zk = source // 8, source % 8
    z, k = zk // 2, zk % 2
    return zk * 4 + x, (x * 2 + k) * 4 + z


def forward_kernel(
    source, target, relation, live, values, mirrors, rel_emb, query_rel, rel_score, out, query_part
):
    step = pl.program_id(0)

    @pl.when(step < query_part.shape[0] // 64)
    def _():
        def pick(i, carry):
            for j in range(8):
                row = step * 64 + i * 8 + j
                query_part[pl.ds(row, 1), :] = rel_score[pl.ds(query_rel[row], 1), :]
            return carry

        lax.fori_loop(0, 8, pick, 0)

    @pl.when(step == 0)
    def _():
        out[...] = jnp.zeros_like(out)

    count = live[0, 0]

    @pl.when(step * GROUP < count)
    def _():
        for j in range(GROUP):
            b = step * GROUP + j
            slots = slots_of(source[0, 0, b])
            t = target[0, 0, b]
            block = values[0, 0, j]
            block = jnp.where(b < count, block, jnp.zeros_like(block))
            row = rel_emb[pl.ds(relation[0, 0, b], 1), :]
            for col in range(2):
                part = slice(256 * col, 256 * col + 256)
                composed = (mirrors[col, slots[col]].astype(F32) - row[:, part]).astype(BF)
                out[t, :, part] += dot(block, composed)


def adjacency_specs(blocks):
    return [SMEM_SPEC] * 4 + [
        pl.BlockSpec((1, 1, GROUP, 128, 128), lambda i: (0, 0, i, 0, 0)),
    ]


def forward(
    adj_source, adj_target, adj_relation, live_blocks, adj_values, mirrors, rel_emb, query_rel, rel_score
):
    blocks = adj_values.shape[2]
    queries, depth = query_rel.shape[0], rel_score.shape[1]
    return pl.pallas_call(
        forward_kernel,
        name="forward_blocks",
        grid=(blocks // GROUP,),
        out_shape=(
            jax.ShapeDtypeStruct((4, 128, depth), F32),
            jax.ShapeDtypeStruct((queries, depth), F32),
        ),
        in_specs=adjacency_specs(blocks) + [VMEM_SPEC] * 2 + [SMEM_SPEC, VMEM_SPEC],
        out_specs=(VMEM_SPEC, VMEM_SPEC),
        compiler_params=pltpu.CompilerParams(vmem_limit_bytes=LIMIT),
    )(
        adj_source, adj_target, adj_relation, live_blocks, adj_values,
        mirrors.reshape(2, 32, 128, 256), rel_emb, query_rel, rel_score,
    )


def backward_kernel(source, target, relation, live, values, agg, tiles_out, rel_out, tiles):
    step = pl.program_id(0)

    @pl.when(step == 0)
    def _():
        def clear(i, carry):
            for col in range(2):
                tiles[col, i] = jnp.zeros((128, 256), F32)
            return carry

        lax.fori_loop(0, 32, clear, 0)
        rel_out[...] = jnp.zeros_like(rel_out)

    count = live[0, 0]

    @pl.when(step * GROUP < count)
    def _():
        for j in range(GROUP):
            b = step * GROUP + j
            slots = slots_of(source[0, 0, b])
            r = pl.ds(relation[0, 0, b], 1)
            block = values[0, 0, j]
            block = jnp.where(b < count, block, jnp.zeros_like(block))
            grad = dot(block, agg[target[0, 0, b]], TN)
            rel_out[r, :] -= jnp.sum(grad, axis=0, keepdims=True)
            for col in range(2):
                tiles[col, slots[col]] += grad[:, 256 * col : 256 * col + 256]

    @pl.when(step == pl.num_programs(0) - 1)
    def _():
        def store(i, carry):
            for col in range(2):
                tiles_out[col, i] = tiles[col, i].astype(BF)
            return carry

        lax.fori_loop(0, 32, store, 0)


def backward(adj_source, adj_target, adj_relation, live_blocks, adj_values, agg_tiles):
    blocks = adj_values.shape[2]
    return pl.pallas_call(
        backward_kernel,
        name="backward_blocks",
        grid=(blocks // GROUP,),
        out_shape=(
            jax.ShapeDtypeStruct((2, 32, 128, 256), BF),
            jax.ShapeDtypeStruct((256, 512), F32),
        ),
        in_specs=adjacency_specs(blocks) + [VMEM_SPEC],
        out_specs=(VMEM_SPEC, VMEM_SPEC),
        scratch_shapes=[pltpu.VMEM((2, 32, 128, 256), F32)],
        compiler_params=pltpu.CompilerParams(vmem_limit_bytes=LIMIT),
    )(adj_source, adj_target, adj_relation, live_blocks, adj_values, agg_tiles)


def middle_kernel(
    n_ar,
    partial, self_part, w_in, query_part, query_head, true_tail, allowed,
    h_out, loss, aggregate, pre_out, agg_tiles,
    share, recv_share, act, queries, q_hi, q_lo, ok, scores, stats, cand_grad, col_sum, head_grad, *rest,
):
    ar_refs, (send_sem, recv_sem) = rest[: 2 * n_ar], rest[2 * n_ar :]
    me = Place()
    enter(ring_devices(me))
    wire = Wire(send_sem, recv_sem)
    head_sum = AllReduce(me, wire, 64, STAGES, ar_refs[:n_ar])
    grad_sum = AllReduce(me, wire, 64, STAGES, ar_refs[n_ar:])
    count = queries.shape[0]
    chunks = count // 128
    scale = 512 ** (-0.5)
    copies = []
    for d in (1, 3, 2):
        other = (me.g + d) % 4
        copies.append(wire.put(partial.at[other], recv_share.at[d - 1], me.peer("y", other)))
    for copy in copies:
        copy.wait_recv()
    total = partial[me.g] + recv_share[0] + recv_share[1] + recv_share[2]
    agg = total.astype(BF)
    aggregate[...] = agg
    activated = jnp.tanh(dot(agg, w_in[...]) + self_part[...])
    act[...] = activated
    h = activated.astype(BF)
    h_out[0] = h
    share[...] = h
    first_row = me.c * 512 + me.g * 128
    block_id = me.c * 4 + me.g

    def rows_match(ids, lanes):
        row_ids = first_row + lax.broadcasted_iota(jnp.int32, (128, 128), 0)
        return row_ids == jnp.broadcast_to(ids[:, lanes], (128, 128))

    def lanes_of(i):
        return pl.ds(pl.multiple_of(i * 128, 128), 128)

    def head_chunk(i, carry):
        pick = rows_match(query_head, lanes_of(i)).astype(F32).T.astype(BF)
        part = dot(pick, share[...]).astype(BF).astype(F32)
        for j in range(4):
            head_sum.part[j, pl.ds(i * 8, 8)] = (
                part[:, 128 * j : 128 * j + 128].reshape(8, 16, 128).astype(BF)
            )
        return carry

    lax.fori_loop(0, chunks, head_chunk, 0)
    head_sum.run()

    h32 = share[...].astype(F32)
    h_sq = jnp.sum(h32 * h32, axis=1, keepdims=True)

    def score_chunk(i, carry):
        lanes = lanes_of(i)
        rows = lanes
        square = jnp.zeros((128, 128), F32)
        for j in range(4):
            cols = slice(128 * j, 128 * j + 128)
            head = head_sum.out[j, pl.ds(i * 8, 8)].astype(F32).reshape(128, 128)
            q = head + query_part[rows, cols]
            queries[rows, cols] = q
            high = q.astype(BF)
            q_hi[rows, cols] = high
            q_lo[rows, cols] = (q - high.astype(F32)).astype(BF)
            square = square + q * q
        q_sq = jnp.sum(square.T, axis=0, keepdims=True)
        cross = dot(share[...], q_hi[rows, :], NT) + dot(share[...], q_lo[rows, :], NT)
        score = -scale * (q_sq + h_sq - 2.0 * cross)
        found = jnp.max(
            jnp.where(allowed[rows, :] == block_id, 1.0, 0.0), axis=1, keepdims=True
        )
        mask = jnp.broadcast_to(found, (128, 128)).T
        ok[:, lanes] = mask
        scores[:, lanes] = score
        seen = jnp.where(mask > 0.5, score, NEG_FILL)
        top = jnp.max(seen, axis=0, keepdims=True)
        weight = jnp.sum(
            jnp.exp(jnp.where(mask > 0.5, score - top, NEG_FILL)), axis=0, keepdims=True
        )
        truth = jnp.sum(
            jnp.where(rows_match(true_tail, lanes), score, 0.0), axis=0, keepdims=True
        )
        stats[0, 0, 0, :, lanes] = top
        stats[0, 0, 1, :, lanes] = weight
        stats[0, 0, 2, :, lanes] = truth
        return carry

    lax.fori_loop(0, chunks, score_chunk, 0)

    for level, axis in enumerate(("core", "y", "x", "z")):
        copies = []
        if axis == "core":
            copies.append(wire.put(stats.at[level, 0], stats.at[level, 1], me.sibling()))
        else:
            for d in (1, 3, 2):
                other = (me.at(axis) + d) % 4
                copies.append(
                    wire.put(stats.at[level, 0], stats.at[level, d], me.peer(axis, other))
                )
        for copy in copies:
            copy.wait_recv()
        members = range(len(copies) + 1)
        tops = [stats[level, m, 0] for m in members]
        top = functools.reduce(jnp.maximum, tops)
        stats[level + 1, 0, 0] = top
        stats[level + 1, 0, 1] = functools.reduce(
            lambda a, b: a + b, [stats[level, m, 1] * jnp.exp(tops[m] - top) for m in members]
        )
        stats[level + 1, 0, 2] = functools.reduce(
            lambda a, b: a + b, [stats[level, m, 2] for m in members]
        )
    row_max = stats[4, 0, 0]
    log_norm = row_max + jnp.log(stats[4, 0, 1])
    loss[...] = log_norm - stats[4, 0, 2]
    stats[4, 1, 0] = log_norm
    stats[4, 1, 1] = (stats[4, 0, 1] * jnp.exp(row_max - log_norm) - 1.0) / count

    cand_grad[...] = jnp.zeros_like(cand_grad)
    col_sum[...] = jnp.zeros_like(col_sum)

    def grad_chunk(i, carry):
        lanes = lanes_of(i)
        norm = jnp.broadcast_to(stats[4, 1, 0, :, lanes], (128, 128))
        prob = jnp.exp(jnp.where(ok[:, lanes] > 0.5, scores[:, lanes] - norm, NEG_FILL))
        tail = jnp.where(rows_match(true_tail, lanes), 1.0, 0.0)
        grad = (prob - tail) / count
        flipped = grad.T
        high = flipped.astype(BF)
        low = (flipped - high.astype(F32)).astype(BF)
        part = dot(high, share[...]) + dot(low, share[...])
        for j in range(4):
            grad_sum.part[j, pl.ds(i * 8, 8)] = (
                part[:, 128 * j : 128 * j + 128].reshape(8, 16, 128).astype(BF)
            )
        high = grad.astype(BF)
        low = (grad - high.astype(F32)).astype(BF)
        cand_grad[...] += (
            dot(high, q_hi[lanes, :]) + dot(high, q_lo[lanes, :]) + dot(low, q_hi[lanes, :])
        )
        col_sum[...] += grad
        return carry

    lax.fori_loop(0, chunks, grad_chunk, 0)
    grad_sum.run()

    head_grad[...] = jnp.zeros_like(head_grad)

    def head_grad_chunk(i, carry):
        lanes = lanes_of(i)
        rest_sum = jnp.broadcast_to(stats[4, 1, 1, :, lanes], (128, 128)).T
        pick = rows_match(query_head, lanes).astype(F32).astype(BF)
        for j in range(4):
            cols = slice(128 * j, 128 * j + 128)
            summed = grad_sum.out[j, pl.ds(i * 8, 8)].astype(F32).reshape(128, 128)
            query_grad = (summed - queries[lanes, cols] * rest_sum).astype(BF)
            head_grad[:, cols] += dot(pick, query_grad)
        return carry

    lax.fori_loop(0, chunks, head_grad_chunk, 0)
    sums = jnp.sum(col_sum[...], axis=1, keepdims=True)
    row_grad = (2.0 * scale) * (
        cand_grad[...] - share[...].astype(F32) * sums + head_grad[...]
    )
    activated = act[...]
    pre_grad = (row_grad * (1.0 - activated * activated)).astype(BF)
    pre_out[...] = pre_grad
    agg_tiles[me.g] = dot(pre_grad, w_in[...], NT).astype(BF)
    copies = []
    for d in (1, 3, 2):
        other = (me.g + d) % 4
        copies.append(wire.put(agg_tiles.at[me.g], agg_tiles.at[me.g], me.peer("y", other)))
    for copy in copies:
        copy.wait_recv()
    wire.drain()


def middle(partial, self_part, w_in, query_part, query_head, true_tail, allowed):
    count = query_head.shape[1]
    depth = w_in.shape[0]
    ar = AllReduce.scratch(64, STAGES)
    copies = 3 + 2 * (1 + 18 + 18 + 1) + 1 + 9 + 3
    return pl.pallas_call(
        functools.partial(middle_kernel, len(ar)),
        name="middle",
        out_shape=(
            jax.ShapeDtypeStruct((1, 128, depth), BF),
            jax.ShapeDtypeStruct((1, count), F32),
            jax.ShapeDtypeStruct((128, depth), BF),
            jax.ShapeDtypeStruct((128, depth), BF),
            jax.ShapeDtypeStruct((4, 128, depth), BF),
        ),
        in_specs=[VMEM_SPEC] * 7,
        out_specs=(VMEM_SPEC,) * 5,
        scratch_shapes=[
            pltpu.VMEM((128, depth), BF),
            pltpu.VMEM((3, 128, depth), F32),
            pltpu.VMEM((128, depth), F32),
            pltpu.VMEM((count, depth), F32),
            pltpu.VMEM((count, depth), BF),
            pltpu.VMEM((count, depth), BF),
            pltpu.VMEM((128, count), F32),
            pltpu.VMEM((128, count), F32),
            pltpu.VMEM((5, 4, 3, 1, count), F32),
            pltpu.VMEM((128, depth), F32),
            pltpu.VMEM((128, 128), F32),
            pltpu.VMEM((128, depth), F32),
            *ar,
            *ar,
            pltpu.SemaphoreType.DMA((copies,)),
            pltpu.SemaphoreType.DMA((copies,)),
        ],
        compiler_params=pltpu.CompilerParams(
            collective_id=1, has_side_effects=True, vmem_limit_bytes=LIMIT
        ),
    )(partial, self_part, w_in, query_part, query_head, true_tail, allowed)


def return_kernel(
    n_w, n_r,
    tiles, rel_part, aggregate, pre_grad, node, w_self, requests,
    node_grad, rel_grad, w_in_grad, w_self_grad,
    arrived, shipped, joined, own_sum, y_send, y_recv, self_grad, *rest,
):
    w_refs, r_refs = rest[:n_w], rest[n_w : n_w + n_r]
    send_sem, recv_sem, local_sem = rest[n_w + n_r :]
    me = Place()
    devices = []
    for e in range(1, 8):
        devices.append(me.dev(me.g, me.x * 8 + (me.zk + e) % 8))
    for e in range(1, 8):
        other = (me.xk + e) % 8
        devices.append(me.dev(me.g, (other // 2) * 8 + me.z * 2 + other % 2))
    for d in (1, 2, 3):
        devices.append(me.peer("y", (me.g + d) % 4))
    enter(devices)
    wire = Wire(send_sem, recv_sem)
    w_sum = AllReduce(me, wire, 64, STAGES, w_refs)
    r_sum = AllReduce(me, wire, 16, STAGES_CAND, r_refs)
    axes = ((0, "x"), (1, "z"))
    order = (1, 3, 2, 0)
    own_slots = (me.zk, me.xk)
    moved = {}
    for d in order:
        for col, axis in axes:
            place = (me.at(axis) + d) % 4
            for e in range(1, 8):
                slot = (own_slots[col] + e) % 8
                moved[d, col, e] = wire.put(
                    tiles.at[col, slot, place],
                    arrived.at[col, own_slots[col], place],
                    devices[7 * col + e - 1],
                )
    local = []
    for col in range(2):
        copy = pltpu.make_async_copy(
            tiles.at[col, own_slots[col]], arrived.at[col, own_slots[col]], local_sem.at[col]
        )
        copy.start()
        local.append(copy)
    own = node[0, pl.ds(pl.multiple_of(me.g * 128, 128), 128), :]
    self_grad[...] = dot(pre_grad[...], w_self[...], NT)
    for at, left in ((0, aggregate[...]), (32, own)):
        for q in range(4):
            turned = left[:, 128 * q : 128 * q + 128].astype(F32).T.astype(BF)
            part = dot(turned, pre_grad[...])
            for j in range(4):
                w_sum.part[j, at + 8 * q : at + 8 * q + 8] = (
                    part[:, 128 * j : 128 * j + 128].reshape(8, 16, 128).astype(BF)
                )
    for q in range(2):
        for j in range(4):
            r_sum.part[j, 8 * q : 8 * q + 8] = (
                rel_part[128 * q : 128 * q + 128, 128 * j : 128 * j + 128]
                .reshape(8, 16, 128)
                .astype(BF)
            )
    for copy in local:
        copy.wait()
    second = []
    for d in order:
        for col, axis in axes:
            place = (me.at(axis) + d) % 4
            owner = place * 8 + me.zk if col == 0 else me.x * 8 + place * 2 + me.k
            for e in range(1, 8):
                moved[d, col, e].wait_recv()
            index = [requests[8 * col + m, 0, owner] for m in range(8)]
            for part in range(4):
                rows = pl.ds(part * 32, 32)
                values = [arrived[col, m, place, rows, :].astype(F32) for m in range(8)]
                for s in range(4):
                    total = jnp.zeros((32, 256), F32)
                    for m in range(8):
                        total = total + jnp.where(index[m] == s, values[m], 0.0)
                    if d == 0:
                        own_sum[col, s, rows, :] = total
                    else:
                        shipped[col, d - 1, s, rows, :] = total.astype(BF)
            if d:
                second.append(
                    wire.put(
                        shipped.at[col, d - 1], joined.at[col, d - 1], me.peer(axis, place)
                    )
                )
    for copy in second:
        copy.wait_recv()
    third = []
    for d in (1, 3, 2, 0):
        s = (me.g + d) % 4
        for col in range(2):
            total = own_sum[col, s]
            for m in range(3):
                total = total + joined[col, m, s].astype(F32)
            if d == 0:
                own_sum[col, s] = total
            else:
                y_send[col, d - 1] = total.astype(BF)
                third.append(
                    wire.put(y_send.at[col, d - 1], y_recv.at[col, d - 1], me.peer("y", s))
                )
    for copy in third:
        copy.wait_recv()
    for col in range(2):
        total = own_sum[col, me.g]
        for m in range(3):
            total = total + y_recv[col, m].astype(F32)
        node_grad[0, :, 256 * col : 256 * col + 256] = (
            total + self_grad[:, 256 * col : 256 * col + 256]
        )
    run_together(w_sum, r_sum)
    for j in range(4):
        cols = slice(128 * j, 128 * j + 128)
        for q in range(4):
            rows = slice(128 * q, 128 * q + 128)
            w_in_grad[rows, cols] = w_sum.out[j, 8 * q : 8 * q + 8].astype(F32).reshape(128, 128)
            w_self_grad[rows, cols] = (
                w_sum.out[j, 32 + 8 * q : 40 + 8 * q].astype(F32).reshape(128, 128)
            )
        both = r_sum.out[j].astype(F32).reshape(256, 128)
        rel_grad[:, cols] = both[: rel_grad.shape[0]]
    wire.drain()


def give_back(tiles, rel_part, aggregate, pre_grad, node_emb, w_self, requests, relations):
    depth = w_self.shape[0]
    w_ar = AllReduce.scratch(64, STAGES)
    r_ar = AllReduce.scratch(16, STAGES_CAND)
    copies = 56 + 6 + 6 + (1 + 18 + 18 + 1) + (1 + 12 + 12 + 1)
    return pl.pallas_call(
        functools.partial(return_kernel, len(w_ar), len(r_ar)),
        name="give_back",
        out_shape=(
            jax.ShapeDtypeStruct((1, 128, depth), F32),
            jax.ShapeDtypeStruct((relations, depth), F32),
            jax.ShapeDtypeStruct((depth, depth), F32),
            jax.ShapeDtypeStruct((depth, depth), F32),
        ),
        in_specs=[ANY_SPEC] + [VMEM_SPEC] * 5 + [SMEM_SPEC],
        out_specs=(VMEM_SPEC,) * 4,
        scratch_shapes=[
            pltpu.VMEM((2, 8, 4, 128, 256), BF),
            pltpu.VMEM((2, 3, 4, 128, 256), BF),
            pltpu.VMEM((2, 3, 4, 128, 256), BF),
            pltpu.VMEM((2, 4, 128, 256), F32),
            pltpu.VMEM((2, 3, 128, 256), BF),
            pltpu.VMEM((2, 3, 128, 256), BF),
            pltpu.VMEM((128, depth), F32),
            *w_ar,
            *r_ar,
            pltpu.SemaphoreType.DMA((copies,)),
            pltpu.SemaphoreType.DMA((copies,)),
            pltpu.SemaphoreType.DMA((2,)),
        ],
        compiler_params=pltpu.CompilerParams(
            collective_id=2, has_side_effects=True, vmem_limit_bytes=LIMIT
        ),
    )(tiles, rel_part, aggregate, pre_grad, node_emb, w_self, requests)


def body(
    node_emb,
    rel_emb,
    w_in,
    w_self,
    rel_score,
    mirror_blocks,
    adj_values,
    adj_source,
    adj_target,
    adj_relation,
    live_blocks,
    query_head,
    query_rel,
    allowed,
    true_tail,
):
    wanted = mirror_blocks.reshape(1, 32)
    mirrors, requests, self_part = fetch(node_emb.reshape(4, 128, -1), wanted, w_self)
    partial, query_part = forward(
        adj_source, adj_target, adj_relation, live_blocks, adj_values, mirrors, rel_emb,
        query_rel, rel_score,
    )
    h_out, loss, aggregate, pre_grad, agg_tiles = middle(
        partial,
        self_part,
        w_in,
        query_part,
        query_head.reshape(1, -1),
        true_tail.reshape(1, -1),
        allowed,
    )
    tiles, rel_part = backward(
        adj_source, adj_target, adj_relation, live_blocks, adj_values, agg_tiles
    )
    node_grad, rel_grad, w_in_grad, w_self_grad = give_back(
        tiles.reshape(2, 8, 4, 128, 256),
        rel_part,
        aggregate,
        pre_grad,
        node_emb,
        w_self,
        requests,
        rel_emb.shape[0],
    )
    return (h_out, loss.reshape(-1), node_grad, rel_grad, w_in_grad, w_self_grad)


def solution(mesh):
    return jax.shard_map(
        body,
        mesh=mesh,
        in_specs=(
            P("cand", None, None),
            P("grp", None),
            P(),
            P(),
            P(),
            P("grp", "cand", None, None),
            P("grp", "cand", None, None, None),
            P("grp", "cand", None),
            P("grp", "cand", None),
            P("grp", "cand", None),
            P("grp", "cand"),
            P(),
            P(),
            P(),
            P(),
        ),
        out_specs=(P("cand", "grp", None), P(), P("cand", "grp", None), P("grp", None), P(), P()),
        check_vma=False,
    )
```

time: 1360 us -> 293 us (0.22)
  waiting for transfers between devices: 637 us -> 0 us
  Pallas kernels: 0 us -> 282 us
  other arithmetic: 240 us -> 0 us
  blocking collectives: 203 us -> 0 us
  matrix products: 130 us -> 0 us
  local copies, waits for them, and re-layouts: 117 us -> 9 us
  starting transfers between devices: 14.7 us -> 0 us
  between operations: 15.1 us -> 1.33 us
    psum x4 -> x0, waiting for transfers between devices: 491 us -> none  [the longest x1 157 us: body(): lax.psum((jnp.dot(aggregate_bf.T, pre_grad, preferred_element_type=jnp.fl...]
    pallas_call x0 -> x5, Pallas kernels: none -> 282 us  [the longest x1 108 us: middle(): pl.pallas_call(functools.partial(middle_kernel, len(ar)), name='middle',...]
    scatter-add x37 -> x0, other arithmetic: 210 us -> none  [the longest x12 115 us: backward_turn(): mirror_grad = mirror_grad.at[source_now].add(composed_grad)]
    dot_general x35 -> x0, matrix products: 130 us -> none  [the longest x12 54.8 us: forward_turn(): jnp.einsum('bij,bjd->bid', values_now, composed, preferred_element_type=j...]
    psum x2 -> x0, blocking collectives: 129 us -> none  [body(): row_total, truth = lax.psum((local_total, truth_part), ('grp', 'cand'))]
    gather x38 -> x0, local copies, waits for them, and re-layouts: 94.4 us -> none  [the longest x12 50.4 us: forward_turn(): jnp.take(mirrors, source_now, axis=0).astype(jnp.float32)]
    all_gather x1 -> x0, waiting for transfers between devices: 71.8 us -> none  [body(): everything = lax.all_gather(node_emb, 'cand', axis=0, tiled=True)]
    pmax x1 -> x0, blocking collectives: 63.8 us -> none  [body(): row_max = lax.pmax(local_max, ('grp', 'cand'))]
  transfers between devices with their start and end apart: 9 -> 0, of which waited for: 7 -> 0; matrix products, arithmetic and copies ran while one was open for 18% -> 0% of each run, Pallas kernels for 0% -> 0%
where the time goes in v1:
time: 293 us; the launch traced here: 292 us
  Pallas kernels  282 us (96%)
  local copies, waits for them, and re-layouts  9 us (3%)
    pallas_call x1, Pallas kernels, middle(): pl.pallas_call(functools.partial(middle_kernel, len(ar)), name='middle',...  108 us
    pallas_call x1, Pallas kernels, give_back(): pl.pallas_call(functools.partial(return_kernel, len(w_ar), len(r_ar)), na...  83 us
    pallas_call x1, Pallas kernels, fetch(): pl.pallas_call(fetch_kernel, name='fetch', out_shape=(jax.ShapeDtypeStruc...  50.7 us
    pallas_call x1, Pallas kernels, forward(): pl.pallas_call(forward_kernel, name='forward_blocks', grid=(blocks // GRO...  21.2 us
    pallas_call x1, Pallas kernels, backward(): pl.pallas_call(backward_kernel, name='backward_blocks', grid=(blocks // G...  19 us
    unnamed x15, local copies, waits for them, and re-layouts  9 us

profile of v1, /device:TPU:1, one launch (start us, length us, event | category | flops | bytes accessed | tf_op | source)
XLA Modules:
  0.0 292.3 jit_solution(13451302285059580126)
XLA Ops:
  1.3 50.7 %fetch.1 = (bf16[2,8,4,128,256]{4,3,2,1,0:T(8,128)(2,1)}, s32[16,1,128]{2,1,0:T(1,128)}, f32[128,512]{1,0:T(8,128)}) custom-call(bf16[4,128,512]{2,1,0:T(8,128)(2,1)} %bitcast.9, s32[1,32]{1,0:T(1,128)} %bitcast.13, bf16[512,512]{1,0:T(8,128)(2,1)} %w_self.3), custom_call_target="tpu_custom_call" | custom-call | tf_op jit(solution)/shard_map/fetch/pallas_call | solution.py:305
  52.0 0.0 copy-start.2
  52.0 21.2 %forward_blocks.1 = (f32[4,128,512]{2,1,0:T(8,128)}, f32[1024,512]{1,0:T(8,128)}) custom-call(s32[1,1,192]{2,1,0:T(1,128)} %source.3, s32[1,1,192]{2,1,0:T(1,128)} %target.3, s32[1,1,192]{2,1,0:T(1,128)} %relation.3, s32[1,1]{1,0:T(1,128)S(6)} %copy.28.live, bf16[1,1,192,128,128]{4,3,2,1,0:T(8,128)(2,1)} %values.3, bf16[2,32,128,256]{3,2,1,0:T(8,128)(2,1)} %bitcast.8, ...), custom_call_target="tpu_custom_call" | custom-call | tf_op jit(solution)/shard_map/forward_blocks/pallas_call | solution.py:386
  73.3 0.0 copy-done.2
  73.3 1.0 copy.21.allowed
  74.3 108.0 %middle.1 = (bf16[1,128,512]{2,1,0:T(8,128)(2,1)}, f32[1,1024]{1,0:T(1,128)}, bf16[128,512]{1,0:T(8,128)(2,1)}, bf16[128,512]{1,0:T(8,128)(2,1)}, bf16[4,128,512]{2,1,0:T(8,128)(2,1)}) custom-call(f32[4,128,512]{2,1,0:T(8,128)} %get-tuple-element.23.partial, f32[128,512]{1,0:T(8,128)} %get-tuple-element.24.self_part, bf16[512,512]{1,0:T(8,128)(2,1)} %w_in.1, ...), custom_call_target="tpu_custom_call" | custom-call | tf_op jit(solution)/shard_map/middle/pallas_call | solution.py:641
  182.2 19.0 %backward_blocks.1 = (bf16[2,32,128,256]{3,2,1,0:T(8,128)(2,1)}, f32[256,512]{1,0:T(8,128)}) custom-call(s32[1,1,192]{2,1,0:T(1,128)} %source.3, s32[1,1,192]{2,1,0:T(1,128)} %target.3, s32[1,1,192]{2,1,0:T(1,128)} %relation.3, s32[1,1]{1,0:T(1,128)S(6)} %copy.28.live, bf16[1,1,192,128,128]{4,3,2,1,0:T(8,128)(2,1)} %values.3, ...), custom_call_target="tpu_custom_call" | custom-call | tf_op jit(solution)/shard_map/backward_blocks/pallas_call | solution.py:443
  201.2 0.0 copy-start.1
  201.2 0.0 copy-start.3
  201.2 83.0 %give_back.1 = (f32[1,128,512]{2,1,0:T(8,128)}, f32[225,512]{1,0:T(8,128)}, f32[512,512]{1,0:T(8,128)}, f32[512,512]{1,0:T(8,128)}) custom-call(bf16[2,8,4,128,256]{4,3,2,1,0:T(8,128)(2,1)} %bitcast.7, f32[256,512]{1,0:T(8,128)} %get-tuple-element.30.rel_part, bf16[128,512]{1,0:T(8,128)(2,1)} %get-tuple-element.31.aggregate, ...), custom_call_target="tpu_custom_call" | custom-call | tf_op jit(solution)/shard_map/give_back/pallas_call | solution.py:807
  284.3 0.0 copy-start
  284.3 0.0 copy-done.1
  284.3 0.7 copy.29
  285.0 0.0 copy-done.3
  285.0 0.6 copy.30
  285.6 1.7 copy.31
  287.2 1.8 copy.32
  289.1 2.3 copy.33
  291.3 0.0 copy-done
  291.3 1.0 copy.34
Async XLA Ops:
  52.0 21.3 %copy-start.2 = (s32[1024,8]{0,1:T(8,128)S(1)}, s32[1024,8]{0,1:T(8,128)}, u32[]{:S(2)}) copy-start(s32[1024,8]{0,1:T(8,128)} %param.28) | copy-start | bytes 98308
  201.2 83.1 %copy-start.1 = (bf16[1,128,512]{2,1,0:T(8,128)(2,1)S(1)}, bf16[1,128,512]{2,1,0:T(8,128)(2,1)}, u32[]{:S(2)}) copy-start(bf16[1,128,512]{2,1,0:T(8,128)(2,1)} %get-tuple-element.44) | copy-start | bytes 393220
  201.2 83.7 %copy-start.3 = (f32[1,1024]{1,0:T(1,128)S(1)}, f32[1,1024]{1,0:T(1,128)}, u32[]{:S(2)}) copy-start(f32[1,1024]{1,0:T(1,128)} %get-tuple-element.27) | copy-start | bytes 12292
  284.3 7.0 %copy-start = (f32[512,512]{1,0:T(8,128)S(1)}, f32[512,512]{1,0:T(8,128)}, u32[]{:S(2)}) copy-start(f32[512,512]{1,0:T(8,128)} %get-tuple-element.49) | copy-start | bytes 3145732

commit v2 on v1

--- a/solution.py
+++ b/solution.py
@@ -18,7 +18,6 @@
 SMEM_SPEC = pl.BlockSpec(memory_space=pltpu.SMEM)
 ANY_SPEC = pl.BlockSpec(memory_space=pl.ANY)
 LIMIT = 60 * 1024 * 1024
-STAGES = (("z", "x", "y"), ("x", "z", "y"))
 STAGES_CAND = (("z", "x"), ("x", "z"))
 
 
@@ -112,16 +111,16 @@
 
 class AllReduce:
     @staticmethod
-    def scratch(shards, stages):
+    def scratch(shards, stages, height):
         depth = len(stages[0])
         shapes = [
-            pltpu.VMEM((4, shards, 16, 128), BF),
-            pltpu.VMEM((2, shards, 16, 128), BF),
-            pltpu.VMEM((4, shards, 16, 128), BF),
+            pltpu.VMEM((4, shards, height, 128), BF),
+            pltpu.VMEM((2, shards, height, 128), BF),
+            pltpu.VMEM((4, shards, height, 128), BF),
         ]
         for level in range(depth):
-            shapes.append(pltpu.VMEM((2, shards // 4**level, 16, 128), BF))
-            shapes.append(pltpu.VMEM((2, 3, shards // 4 ** (level + 1), 16, 128), BF))
+            shapes.append(pltpu.VMEM((2, shards // 4**level, height, 128), BF))
+            shapes.append(pltpu.VMEM((2, 3, shards // 4 ** (level + 1), height, 128), BF))
         return shapes
 
     def __init__(self, me, wire, shards, stages, refs):
@@ -200,27 +199,6 @@
             yield
             for copy in copies:
                 copy.wait_recv()
-        place = self.out.at[pl.ds(mine, 2)]
-        copy = wire.put(place, place, me.sibling())
-        yield
-        copy.wait_recv()
-
-    def run(self):
-        for ignored in self.steps():
-            pass
-
-
-def run_together(*reduces):
-    live = [r.steps() for r in reduces]
-    while live:
-        still = []
-        for steps in live:
-            try:
-                next(steps)
-                still.append(steps)
-            except StopIteration:
-                pass
-        live = still
 
 
 def fetch_kernel(
@@ -337,19 +315,17 @@
 
 
 def forward_kernel(
-    source, target, relation, live, values, mirrors, rel_emb, query_rel, rel_score, out, query_part
+    source, target, relation, live, values, mirrors, rel_emb, query_rel, rel_score,
+    out, out_low, query_part,
 ):
     step = pl.program_id(0)
-
-    @pl.when(step < query_part.shape[0] // 64)
+    first = (lax.axis_index("grp") * 2 + lax.axis_index("cand") % 2) * 128
+
+    @pl.when(step < 16)
     def _():
-        def pick(i, carry):
-            for j in range(8):
-                row = step * 64 + i * 8 + j
-                query_part[pl.ds(row, 1), :] = rel_score[pl.ds(query_rel[row], 1), :]
-            return carry
-
-        lax.fori_loop(0, 8, pick, 0)
+        for j in range(8):
+            row = step * 8 + j
+            query_part[pl.ds(row, 1), :] = rel_score[pl.ds(query_rel[first + row], 1), :]
 
     @pl.when(step == 0)
     def _():
@@ -371,6 +347,11 @@
                 composed = (mirrors[col, slots[col]].astype(F32) - row[:, part]).astype(BF)
                 out[t, :, part] += dot(block, composed)
 
+    @pl.when(step == pl.num_programs(0) - 1)
+    def _():
+        for t in range(4):
+            out_low[t] = out[t].astype(BF)
+
 
 def adjacency_specs(blocks):
     return [SMEM_SPEC] * 4 + [
@@ -382,17 +363,18 @@
     adj_source, adj_target, adj_relation, live_blocks, adj_values, mirrors, rel_emb, query_rel, rel_score
 ):
     blocks = adj_values.shape[2]
-    queries, depth = query_rel.shape[0], rel_score.shape[1]
+    depth = rel_score.shape[1]
     return pl.pallas_call(
         forward_kernel,
         name="forward_blocks",
         grid=(blocks // GROUP,),
         out_shape=(
             jax.ShapeDtypeStruct((4, 128, depth), F32),
-            jax.ShapeDtypeStruct((queries, depth), F32),
+            jax.ShapeDtypeStruct((4, 128, depth), BF),
+            jax.ShapeDtypeStruct((128, depth), F32),
         ),
         in_specs=adjacency_specs(blocks) + [VMEM_SPEC] * 2 + [SMEM_SPEC, VMEM_SPEC],
-        out_specs=(VMEM_SPEC, VMEM_SPEC),
+        out_specs=(VMEM_SPEC,) * 3,
         compiler_params=pltpu.CompilerParams(vmem_limit_bytes=LIMIT),
     )(
         adj_source, adj_target, adj_relation, live_blocks, adj_values,
@@ -455,233 +437,293 @@
     )(adj_source, adj_target, adj_relation, live_blocks, adj_values, agg_tiles)
 
 
+def exchange_sum(me, wire, send, recv, out, during=None):
+    for level in range(2):
+        copies = []
+        for d in (1, 3, 2):
+            for col in range(2):
+                axis = STAGES_CAND[col][level]
+                other = (me.at(axis) + d) % 4
+                copies.append(
+                    wire.put(
+                        send.at[level, col], recv.at[level, col, d - 1], me.peer(axis, other)
+                    )
+                )
+        if level == 0 and during is not None:
+            during()
+        for copy in copies:
+            copy.wait_recv()
+        for col in range(2):
+            total = send[level, col].astype(F32)
+            for d in range(3):
+                total = total + recv[level, col, d].astype(F32)
+            if level == 0:
+                send[1, col] = total.astype(BF)
+            else:
+                out[:, 256 * col : 256 * col + 256] = total
+
+
 def middle_kernel(
-    n_ar,
-    partial, self_part, w_in, query_part, query_head, true_tail, allowed,
-    h_out, loss, aggregate, pre_out, agg_tiles,
-    share, recv_share, act, queries, q_hi, q_lo, ok, scores, stats, cand_grad, col_sum, head_grad, *rest,
+    partial_low, partial, self_part, w_in, query_part, query_head, true_tail, allowed,
+    h_out, loss, agg_all, pre_all, agg_tiles,
+    share_recv, act, column, head_send, head_recv, queries, q_hi, q_lo, scores, stats,
+    grad_send, grad_recv, summed, g_hi, g_lo, rows, core_send, core_recv, y_send, y_recv,
+    send_sem, recv_sem,
 ):
-    ar_refs, (send_sem, recv_sem) = rest[: 2 * n_ar], rest[2 * n_ar :]
     me = Place()
     enter(ring_devices(me))
     wire = Wire(send_sem, recv_sem)
-    head_sum = AllReduce(me, wire, 64, STAGES, ar_refs[:n_ar])
-    grad_sum = AllReduce(me, wire, 64, STAGES, ar_refs[n_ar:])
-    count = queries.shape[0]
-    chunks = count // 128
+    count = true_tail.shape[1]
     scale = 512 ** (-0.5)
+    group = me.g * 2 + me.k
+    lanes = pl.ds(pl.multiple_of(group * 128, 128), 128)
+    first_chip = me.x * 8 + me.z * 2
+    base = first_chip * 512
+
+    def to_y(ref, at, order=(1, 3, 2)):
+        copies = {}
+        for d in order:
+            copies[d] = wire.put(ref.at[at], ref.at[at], me.peer("y", (me.g + d) % 4))
+        return copies
+
     copies = []
     for d in (1, 3, 2):
         other = (me.g + d) % 4
-        copies.append(wire.put(partial.at[other], recv_share.at[d - 1], me.peer("y", other)))
+        copies.append(wire.put(partial_low.at[other], share_recv.at[d - 1], me.peer("y", other)))
     for copy in copies:
         copy.wait_recv()
-    total = partial[me.g] + recv_share[0] + recv_share[1] + recv_share[2]
+    total = partial[me.g]
+    for d in range(3):
+        total = total + share_recv[d].astype(F32)
     agg = total.astype(BF)
-    aggregate[...] = agg
     activated = jnp.tanh(dot(agg, w_in[...]) + self_part[...])
+    h = activated.astype(BF)
+    own_chunk = me.k * 4 + me.g
+    column[own_chunk] = h
+    from_y = to_y(column, own_chunk)
+    from_sibling = [wire.put(column.at[own_chunk], column.at[own_chunk], me.sibling())]
+    h_out[0] = h
     act[...] = activated
-    h = activated.astype(BF)
-    h_out[0] = h
-    share[...] = h
-    first_row = me.c * 512 + me.g * 128
-    block_id = me.c * 4 + me.g
-
-    def rows_match(ids, lanes):
-        row_ids = first_row + lax.broadcasted_iota(jnp.int32, (128, 128), 0)
-        return row_ids == jnp.broadcast_to(ids[:, lanes], (128, 128))
-
-    def lanes_of(i):
-        return pl.ds(pl.multiple_of(i * 128, 128), 128)
-
-    def head_chunk(i, carry):
-        pick = rows_match(query_head, lanes_of(i)).astype(F32).T.astype(BF)
-        part = dot(pick, share[...]).astype(BF).astype(F32)
-        for j in range(4):
-            head_sum.part[j, pl.ds(i * 8, 8)] = (
-                part[:, 128 * j : 128 * j + 128].reshape(8, 16, 128).astype(BF)
+    agg_all[me.g] = agg
+    agg_copies = to_y(agg_all, me.g)
+    for d in (1, 3, 2):
+        from_y[d].wait_recv()
+        chunk = me.k * 4 + (me.g + 4 - d) % 4
+        from_sibling.append(wire.put(column.at[chunk], column.at[chunk], me.sibling()))
+
+    head_row = jnp.broadcast_to(query_head[:, lanes] - base, (128, 128))
+    head_col = head_row.astype(F32).T
+    lane_ids = lax.broadcasted_iota(jnp.int32, (128, 128), 1).astype(F32)
+    row_ids = lax.broadcasted_iota(jnp.int32, (128, 128), 0)
+    for copy in from_sibling:
+        copy.wait_recv()
+    part = jnp.zeros((128, 512), F32)
+    for j in range(8):
+        pick = jnp.where(head_col == lane_ids + 128.0 * j, 1.0, 0.0).astype(BF)
+        part = part + dot(pick, column[j])
+    for col in range(2):
+        head_send[0, col] = part[:, 256 * col : 256 * col + 256].astype(BF)
+    exchange_sum(me, wire, head_send, head_recv, summed)
+
+    q = summed[...] + query_part[...]
+    queries[...] = q
+    high = q.astype(BF)
+    q_hi[...] = high
+    q_lo[...] = (q - high.astype(F32)).astype(BF)
+    square = jnp.zeros((128, 128), F32)
+    for j in range(4):
+        piece = q[:, 128 * j : 128 * j + 128]
+        square = square + piece * piece
+    q_sq = jnp.sum(square.T, axis=0, keepdims=True)
+    tail_row = jnp.broadcast_to(true_tail[:, lanes] - base, (128, 128))
+    kinds = allowed[:, lanes]
+
+    def allowed_row(j):
+        hit = jnp.where(kinds == first_chip * 4 + j, 1.0, 0.0)
+        return jnp.max(hit, axis=0, keepdims=True)
+
+    masks = [jnp.broadcast_to(allowed_row(j), (128, 128)) > 0.5 for j in range(8)]
+    tops, truths = [], []
+    for j in range(8):
+        h32 = column[j].astype(F32)
+        h_sq = jnp.sum(h32 * h32, axis=1, keepdims=True)
+        cross = dot(column[j], q_hi[...], NT) + dot(column[j], q_lo[...], NT)
+        score = -scale * (q_sq + h_sq - 2.0 * cross)
+        scores[j] = score
+        tops.append(jnp.max(jnp.where(masks[j], score, NEG_FILL), axis=0, keepdims=True))
+        truths.append(
+            jnp.sum(
+                jnp.where(row_ids + 128 * j == tail_row, score, 0.0), axis=0, keepdims=True
             )
-        return carry
-
-    lax.fori_loop(0, chunks, head_chunk, 0)
-    head_sum.run()
-
-    h32 = share[...].astype(F32)
-    h_sq = jnp.sum(h32 * h32, axis=1, keepdims=True)
-
-    def score_chunk(i, carry):
-        lanes = lanes_of(i)
-        rows = lanes
-        square = jnp.zeros((128, 128), F32)
-        for j in range(4):
-            cols = slice(128 * j, 128 * j + 128)
-            head = head_sum.out[j, pl.ds(i * 8, 8)].astype(F32).reshape(128, 128)
-            q = head + query_part[rows, cols]
-            queries[rows, cols] = q
-            high = q.astype(BF)
-            q_hi[rows, cols] = high
-            q_lo[rows, cols] = (q - high.astype(F32)).astype(BF)
-            square = square + q * q
-        q_sq = jnp.sum(square.T, axis=0, keepdims=True)
-        cross = dot(share[...], q_hi[rows, :], NT) + dot(share[...], q_lo[rows, :], NT)
-        score = -scale * (q_sq + h_sq - 2.0 * cross)
-        found = jnp.max(
-            jnp.where(allowed[rows, :] == block_id, 1.0, 0.0), axis=1, keepdims=True
         )
-        mask = jnp.broadcast_to(found, (128, 128)).T
-        ok[:, lanes] = mask
-        scores[:, lanes] = score
-        seen = jnp.where(mask > 0.5, score, NEG_FILL)
-        top = jnp.max(seen, axis=0, keepdims=True)
-        weight = jnp.sum(
-            jnp.exp(jnp.where(mask > 0.5, score - top, NEG_FILL)), axis=0, keepdims=True
+    top = functools.reduce(jnp.maximum, tops)
+    weight = jnp.zeros((1, 128), F32)
+    for j in range(8):
+        weight = weight + jnp.sum(
+            jnp.exp(jnp.where(masks[j], scores[j] - top, NEG_FILL)), axis=0, keepdims=True
         )
-        truth = jnp.sum(
-            jnp.where(rows_match(true_tail, lanes), score, 0.0), axis=0, keepdims=True
-        )
-        stats[0, 0, 0, :, lanes] = top
-        stats[0, 0, 1, :, lanes] = weight
-        stats[0, 0, 2, :, lanes] = truth
-        return carry
-
-    lax.fori_loop(0, chunks, score_chunk, 0)
-
-    for level, axis in enumerate(("core", "y", "x", "z")):
+    stats[0, 0, 0:1, :] = top
+    stats[0, 0, 1:2, :] = weight
+    stats[0, 0, 2:3, :] = functools.reduce(lambda a, b: a + b, truths)
+
+    for level, axis in enumerate(("z", "x")):
         copies = []
-        if axis == "core":
-            copies.append(wire.put(stats.at[level, 0], stats.at[level, 1], me.sibling()))
-        else:
-            for d in (1, 3, 2):
-                other = (me.at(axis) + d) % 4
-                copies.append(
-                    wire.put(stats.at[level, 0], stats.at[level, d], me.peer(axis, other))
-                )
+        for d in (1, 3, 2):
+            other = (me.at(axis) + d) % 4
+            copies.append(wire.put(stats.at[level, 0], stats.at[level, d], me.peer(axis, other)))
         for copy in copies:
             copy.wait_recv()
-        members = range(len(copies) + 1)
-        tops = [stats[level, m, 0] for m in members]
+        members = [stats[level, m] for m in range(4)]
+        tops = [m[0:1, :] for m in members]
         top = functools.reduce(jnp.maximum, tops)
-        stats[level + 1, 0, 0] = top
-        stats[level + 1, 0, 1] = functools.reduce(
-            lambda a, b: a + b, [stats[level, m, 1] * jnp.exp(tops[m] - top) for m in members]
-        )
-        stats[level + 1, 0, 2] = functools.reduce(
-            lambda a, b: a + b, [stats[level, m, 2] for m in members]
-        )
-    row_max = stats[4, 0, 0]
-    log_norm = row_max + jnp.log(stats[4, 0, 1])
-    loss[...] = log_norm - stats[4, 0, 2]
-    stats[4, 1, 0] = log_norm
-    stats[4, 1, 1] = (stats[4, 0, 1] * jnp.exp(row_max - log_norm) - 1.0) / count
-
-    cand_grad[...] = jnp.zeros_like(cand_grad)
-    col_sum[...] = jnp.zeros_like(col_sum)
-
-    def grad_chunk(i, carry):
-        lanes = lanes_of(i)
-        norm = jnp.broadcast_to(stats[4, 1, 0, :, lanes], (128, 128))
-        prob = jnp.exp(jnp.where(ok[:, lanes] > 0.5, scores[:, lanes] - norm, NEG_FILL))
-        tail = jnp.where(rows_match(true_tail, lanes), 1.0, 0.0)
+        weight = members[0][1:2, :] * jnp.exp(tops[0] - top)
+        truth = members[0][2:3, :]
+        for m in range(1, 4):
+            weight = weight + members[m][1:2, :] * jnp.exp(tops[m] - top)
+            truth = truth + members[m][2:3, :]
+        if level == 0:
+            stats[1, 0, 0:1, :] = top
+            stats[1, 0, 1:2, :] = weight
+            stats[1, 0, 2:3, :] = truth
+    log_norm = top + jnp.log(weight)
+    loss[group] = log_norm - truth
+    loss_copies = to_y(loss, group)
+    rest_sum = (weight * jnp.exp(top - log_norm) - 1.0) / count
+    rest_col = jnp.broadcast_to(rest_sum, (128, 128)).T
+
+    part = jnp.zeros((128, 512), F32)
+    for j in range(8):
+        prob = jnp.exp(jnp.where(masks[j], scores[j] - log_norm, NEG_FILL))
+        tail = jnp.where(row_ids + 128 * j == tail_row, 1.0, 0.0)
         grad = (prob - tail) / count
+        scores[j] = grad
+        high = grad.astype(BF)
+        g_hi[j] = high
+        g_lo[j] = (grad - high.astype(F32)).astype(BF)
         flipped = grad.T
         high = flipped.astype(BF)
         low = (flipped - high.astype(F32)).astype(BF)
-        part = dot(high, share[...]) + dot(low, share[...])
-        for j in range(4):
-            grad_sum.part[j, pl.ds(i * 8, 8)] = (
-                part[:, 128 * j : 128 * j + 128].reshape(8, 16, 128).astype(BF)
+        part = part + (dot(high, column[j]) + dot(low, column[j]))
+    for col in range(2):
+        grad_send[0, col] = part[:, 256 * col : 256 * col + 256].astype(BF)
+
+    def candidates():
+        for j in range(8):
+            sums = jnp.sum(scores[j], axis=1, keepdims=True)
+            rows[j] = (
+                dot(g_hi[j], q_hi[...]) + dot(g_hi[j], q_lo[...]) + dot(g_lo[j], q_hi[...])
+            ) - column[j].astype(F32) * sums
+
+    exchange_sum(me, wire, grad_send, grad_recv, summed, candidates)
+
+    query_grad = jnp.concatenate(
+        [
+            summed[:, 128 * j : 128 * j + 128] - queries[:, 128 * j : 128 * j + 128] * rest_col
+            for j in range(4)
+        ],
+        axis=1,
+    ).astype(BF)
+
+    def row_part(chunk):
+        pick = jnp.where(row_ids + 128 * chunk == head_row, 1.0, 0.0).astype(BF)
+        return rows[chunk] + dot(pick, query_grad)
+
+    order = (1, 3, 2, 0)
+    core_copies = {}
+    for at, d in enumerate(order):
+        chunk = (1 - me.k) * 4 + (me.g + d) % 4
+        core_send[d] = row_part(chunk).astype(BF)
+        core_copies[d] = wire.put(core_send.at[d], core_recv.at[d], me.sibling())
+    y_copies = []
+    for d in order:
+        own = row_part(me.k * 4 + (me.g + d) % 4)
+        core_copies[d].wait_recv()
+        total = own + core_recv[d].astype(F32)
+        if d:
+            y_send[d - 1] = total.astype(BF)
+            y_copies.append(
+                wire.put(y_send.at[d - 1], y_recv.at[d - 1], me.peer("y", (me.g + d) % 4))
             )
-        high = grad.astype(BF)
-        low = (grad - high.astype(F32)).astype(BF)
-        cand_grad[...] += (
-            dot(high, q_hi[lanes, :]) + dot(high, q_lo[lanes, :]) + dot(low, q_hi[lanes, :])
-        )
-        col_sum[...] += grad
-        return carry
-
-    lax.fori_loop(0, chunks, grad_chunk, 0)
-    grad_sum.run()
-
-    head_grad[...] = jnp.zeros_like(head_grad)
-
-    def head_grad_chunk(i, carry):
-        lanes = lanes_of(i)
-        rest_sum = jnp.broadcast_to(stats[4, 1, 1, :, lanes], (128, 128)).T
-        pick = rows_match(query_head, lanes).astype(F32).astype(BF)
-        for j in range(4):
-            cols = slice(128 * j, 128 * j + 128)
-            summed = grad_sum.out[j, pl.ds(i * 8, 8)].astype(F32).reshape(128, 128)
-            query_grad = (summed - queries[lanes, cols] * rest_sum).astype(BF)
-            head_grad[:, cols] += dot(pick, query_grad)
-        return carry
-
-    lax.fori_loop(0, chunks, head_grad_chunk, 0)
-    sums = jnp.sum(col_sum[...], axis=1, keepdims=True)
-    row_grad = (2.0 * scale) * (
-        cand_grad[...] - share[...].astype(F32) * sums + head_grad[...]
-    )
+    for d in (1, 3, 2):
+        loss_copies[d].wait_recv()
+    loss_rows = []
+    for d in range(4):
+        row = ((me.g + d) % 4) * 2 + me.k
+        loss_rows.append(wire.put(loss.at[row], loss.at[row], me.sibling()))
+    for copy in y_copies:
+        copy.wait_recv()
+    for d in range(3):
+        total = total + y_recv[d].astype(F32)
     activated = act[...]
-    pre_grad = (row_grad * (1.0 - activated * activated)).astype(BF)
-    pre_out[...] = pre_grad
+    pre_grad = (((2.0 * scale) * total) * (1.0 - activated * activated)).astype(BF)
+    pre_all[me.g] = pre_grad
+    pre_copies = to_y(pre_all, me.g)
     agg_tiles[me.g] = dot(pre_grad, w_in[...], NT).astype(BF)
-    copies = []
     for d in (1, 3, 2):
-        other = (me.g + d) % 4
-        copies.append(wire.put(agg_tiles.at[me.g], agg_tiles.at[me.g], me.peer("y", other)))
-    for copy in copies:
+        pre_copies[d].wait_recv()
+        other = (me.g + 4 - d) % 4
+        agg_tiles[other] = dot(pre_all[other], w_in[...], NT).astype(BF)
+    for d in (1, 3, 2):
+        agg_copies[d].wait_recv()
+    for copy in loss_rows:
         copy.wait_recv()
     wire.drain()
 
 
-def middle(partial, self_part, w_in, query_part, query_head, true_tail, allowed):
-    count = query_head.shape[1]
+def middle(partial_low, partial, self_part, w_in, query_part, query_head, true_tail, allowed):
     depth = w_in.shape[0]
-    ar = AllReduce.scratch(64, STAGES)
-    copies = 3 + 2 * (1 + 18 + 18 + 1) + 1 + 9 + 3
+    copies = 64
+    tile_bf = jax.ShapeDtypeStruct((4, 128, depth), BF)
     return pl.pallas_call(
-        functools.partial(middle_kernel, len(ar)),
+        middle_kernel,
         name="middle",
         out_shape=(
             jax.ShapeDtypeStruct((1, 128, depth), BF),
-            jax.ShapeDtypeStruct((1, count), F32),
-            jax.ShapeDtypeStruct((128, depth), BF),
-            jax.ShapeDtypeStruct((128, depth), BF),
-            jax.ShapeDtypeStruct((4, 128, depth), BF),
+            jax.ShapeDtypeStruct((8, 1, 128), F32),
+            tile_bf,
+            tile_bf,
+            tile_bf,
         ),
-        in_specs=[VMEM_SPEC] * 7,
+        in_specs=[VMEM_SPEC] * 8,
         out_specs=(VMEM_SPEC,) * 5,
         scratch_shapes=[
+            pltpu.VMEM((3, 128, depth), BF),
+            pltpu.VMEM((128, depth), F32),
+            pltpu.VMEM((8, 128, depth), BF),
+            pltpu.VMEM((2, 2, 128, 256), BF),
+            pltpu.VMEM((2, 2, 3, 128, 256), BF),
+            pltpu.VMEM((128, depth), F32),
             pltpu.VMEM((128, depth), BF),
-            pltpu.VMEM((3, 128, depth), F32),
+            pltpu.VMEM((128, depth), BF),
+            pltpu.VMEM((8, 128, 128), F32),
+            pltpu.VMEM((2, 4, 8, 128), F32),
+            pltpu.VMEM((2, 2, 128, 256), BF),
+            pltpu.VMEM((2, 2, 3, 128, 256), BF),
             pltpu.VMEM((128, depth), F32),
-            pltpu.VMEM((count, depth), F32),
-            pltpu.VMEM((count, depth), BF),
-            pltpu.VMEM((count, depth), BF),
-            pltpu.VMEM((128, count), F32),
-            pltpu.VMEM((128, count), F32),
-            pltpu.VMEM((5, 4, 3, 1, count), F32),
-            pltpu.VMEM((128, depth), F32),
-            pltpu.VMEM((128, 128), F32),
-            pltpu.VMEM((128, depth), F32),
-            *ar,
-            *ar,
+            pltpu.VMEM((8, 128, 128), BF),
+            pltpu.VMEM((8, 128, 128), BF),
+            pltpu.VMEM((8, 128, depth), F32),
+            pltpu.VMEM((4, 128, depth), BF),
+            pltpu.VMEM((4, 128, depth), BF),
+            pltpu.VMEM((3, 128, depth), BF),
+            pltpu.VMEM((3, 128, depth), BF),
             pltpu.SemaphoreType.DMA((copies,)),
             pltpu.SemaphoreType.DMA((copies,)),
         ],
         compiler_params=pltpu.CompilerParams(
             collective_id=1, has_side_effects=True, vmem_limit_bytes=LIMIT
         ),
-    )(partial, self_part, w_in, query_part, query_head, true_tail, allowed)
+    )(partial_low, partial, self_part, w_in, query_part, query_head, true_tail, allowed)
 
 
 def return_kernel(
-    n_w, n_r,
-    tiles, rel_part, aggregate, pre_grad, node, w_self, requests,
+    n_ar,
+    tiles, rel_part, agg_all, pre_all, node, w_self, requests,
     node_grad, rel_grad, w_in_grad, w_self_grad,
-    arrived, shipped, joined, own_sum, y_send, y_recv, self_grad, *rest,
+    arrived, shipped, joined, own_sum, y_send, y_recv, self_grad, w_all, *rest,
 ):
-    w_refs, r_refs = rest[:n_w], rest[n_w : n_w + n_r]
-    send_sem, recv_sem, local_sem = rest[n_w + n_r :]
+    ar_refs = rest[:n_ar]
+    send_sem, recv_sem, local_sem = rest[n_ar:]
     me = Place()
     devices = []
     for e in range(1, 8):
@@ -693,13 +735,18 @@
         devices.append(me.peer("y", (me.g + d) % 4))
     enter(devices)
     wire = Wire(send_sem, recv_sem)
-    w_sum = AllReduce(me, wire, 64, STAGES, w_refs)
-    r_sum = AllReduce(me, wire, 16, STAGES_CAND, r_refs)
+    reduce = AllReduce(me, wire, 16, STAGES_CAND, ar_refs)
+    steps = reduce.steps()
+
+    def advance():
+        next(steps, None)
+
     axes = ((0, "x"), (1, "z"))
     order = (1, 3, 2, 0)
     own_slots = (me.zk, me.xk)
     moved = {}
-    for d in order:
+
+    def send_round(d):
         for col, axis in axes:
             place = (me.at(axis) + d) % 4
             for e in range(1, 8):
@@ -709,6 +756,9 @@
                     arrived.at[col, own_slots[col], place],
                     devices[7 * col + e - 1],
                 )
+
+    send_round(order[0])
+    send_round(order[1])
     local = []
     for col in range(2):
         copy = pltpu.make_async_copy(
@@ -716,27 +766,30 @@
         )
         copy.start()
         local.append(copy)
-    own = node[0, pl.ds(pl.multiple_of(me.g * 128, 128), 128), :]
-    self_grad[...] = dot(pre_grad[...], w_self[...], NT)
-    for at, left in ((0, aggregate[...]), (32, own)):
+    cols = pl.ds(pl.multiple_of(me.g * 128, 128), 128)
+    right = pre_all[:, :, cols].reshape(512, 128)
+    for which, left in ((0, agg_all), (1, node)):
         for q in range(4):
-            turned = left[:, 128 * q : 128 * q + 128].astype(F32).T.astype(BF)
-            part = dot(turned, pre_grad[...])
-            for j in range(4):
-                w_sum.part[j, at + 8 * q : at + 8 * q + 8] = (
-                    part[:, 128 * j : 128 * j + 128].reshape(8, 16, 128).astype(BF)
-                )
+            turned = left[:, :, 128 * q : 128 * q + 128].astype(F32).reshape(512, 128).T.astype(BF)
+            reduce.part[2 * which + q // 2, 8 * (q % 2) : 8 * (q % 2) + 8, 0:16] = (
+                dot(turned, right).reshape(8, 16, 128).astype(BF)
+            )
     for q in range(2):
         for j in range(4):
-            r_sum.part[j, 8 * q : 8 * q + 8] = (
+            reduce.part[j, 8 * q : 8 * q + 8, 16:32] = (
                 rel_part[128 * q : 128 * q + 128, 128 * j : 128 * j + 128]
                 .reshape(8, 16, 128)
                 .astype(BF)
             )
+    advance()
+    self_grad[...] = dot(pre_all[me.g], w_self[...], NT)
+    advance()
     for copy in local:
         copy.wait()
     second = []
-    for d in order:
+    for at, d in enumerate(order):
+        if at + 2 < 4:
+            send_round(order[at + 2])
         for col, axis in axes:
             place = (me.at(axis) + d) % 4
             owner = place * 8 + me.zk if col == 0 else me.x * 8 + place * 2 + me.k
@@ -760,6 +813,7 @@
                         shipped.at[col, d - 1], joined.at[col, d - 1], me.peer(axis, place)
                     )
                 )
+        advance()
     for copy in second:
         copy.wait_recv()
     third = []
@@ -776,6 +830,19 @@
                 third.append(
                     wire.put(y_send.at[col, d - 1], y_recv.at[col, d - 1], me.peer("y", s))
                 )
+    advance()
+    advance()
+    mine = 2 * me.k
+    pair = pl.ds(mine, 2)
+    both = wire.put(reduce.out.at[pair], reduce.out.at[pair], me.sibling())
+    for col in range(2):
+        w_all[me.g, mine + col] = reduce.out[mine + col, :, 0:16]
+    w_copies = {}
+    for d in (1, 3, 2):
+        w_copies[d] = wire.put(
+            w_all.at[me.g, pair], w_all.at[me.g, pair], me.peer("y", (me.g + d) % 4)
+        )
+    w_rows = [wire.put(w_all.at[me.g, pair], w_all.at[me.g, pair], me.sibling())]
     for copy in third:
         copy.wait_recv()
     for col in range(2):
@@ -785,27 +852,32 @@
         node_grad[0, :, 256 * col : 256 * col + 256] = (
             total + self_grad[:, 256 * col : 256 * col + 256]
         )
-    run_together(w_sum, r_sum)
+    for d in (1, 3, 2):
+        w_copies[d].wait_recv()
+        other = (me.g + 4 - d) % 4
+        w_rows.append(wire.put(w_all.at[other, pair], w_all.at[other, pair], me.sibling()))
+    both.wait_recv()
     for j in range(4):
-        cols = slice(128 * j, 128 * j + 128)
-        for q in range(4):
-            rows = slice(128 * q, 128 * q + 128)
-            w_in_grad[rows, cols] = w_sum.out[j, 8 * q : 8 * q + 8].astype(F32).reshape(128, 128)
-            w_self_grad[rows, cols] = (
-                w_sum.out[j, 32 + 8 * q : 40 + 8 * q].astype(F32).reshape(128, 128)
-            )
-        both = r_sum.out[j].astype(F32).reshape(256, 128)
-        rel_grad[:, cols] = both[: rel_grad.shape[0]]
+        whole = reduce.out[j, :, 16:32].astype(F32).reshape(256, 128)
+        rel_grad[:, 128 * j : 128 * j + 128] = whole[: rel_grad.shape[0]]
+    for copy in w_rows:
+        copy.wait_recv()
+    for j in range(4):
+        for q in range(2):
+            rows = slice(256 * q, 256 * q + 256)
+            for at, target in ((q, w_in_grad), (2 + q, w_self_grad)):
+                target[rows, 128 * j : 128 * j + 128] = (
+                    w_all[j, at].astype(F32).reshape(256, 128)
+                )
     wire.drain()
 
 
-def give_back(tiles, rel_part, aggregate, pre_grad, node_emb, w_self, requests, relations):
+def give_back(tiles, rel_part, agg_all, pre_all, node_tiles, w_self, requests, relations):
     depth = w_self.shape[0]
-    w_ar = AllReduce.scratch(64, STAGES)
-    r_ar = AllReduce.scratch(16, STAGES_CAND)
-    copies = 56 + 6 + 6 + (1 + 18 + 18 + 1) + (1 + 12 + 12 + 1)
+    ar = AllReduce.scratch(16, STAGES_CAND, 32)
+    copies = 56 + 6 + 6 + (1 + 12 + 12) + 1 + 3 + 4
     return pl.pallas_call(
-        functools.partial(return_kernel, len(w_ar), len(r_ar)),
+        functools.partial(return_kernel, len(ar)),
         name="give_back",
         out_shape=(
             jax.ShapeDtypeStruct((1, 128, depth), F32),
@@ -823,8 +895,8 @@
             pltpu.VMEM((2, 3, 128, 256), BF),
             pltpu.VMEM((2, 3, 128, 256), BF),
             pltpu.VMEM((128, depth), F32),
-            *w_ar,
-            *r_ar,
+            pltpu.VMEM((4, 4, 16, 16, 128), BF),
+            *ar,
             pltpu.SemaphoreType.DMA((copies,)),
             pltpu.SemaphoreType.DMA((copies,)),
             pltpu.SemaphoreType.DMA((2,)),
@@ -832,7 +904,7 @@
         compiler_params=pltpu.CompilerParams(
             collective_id=2, has_side_effects=True, vmem_limit_bytes=LIMIT
         ),
-    )(tiles, rel_part, aggregate, pre_grad, node_emb, w_self, requests)
+    )(tiles, rel_part, agg_all, pre_all, node_tiles, w_self, requests)
 
 
 def body(
@@ -853,19 +925,21 @@
     true_tail,
 ):
     wanted = mirror_blocks.reshape(1, 32)
-    mirrors, requests, self_part = fetch(node_emb.reshape(4, 128, -1), wanted, w_self)
-    partial, query_part = forward(
+    node_tiles = node_emb.reshape(4, 128, -1)
+    mirrors, requests, self_part = fetch(node_tiles, wanted, w_self)
+    partial, partial_low, query_part = forward(
         adj_source, adj_target, adj_relation, live_blocks, adj_values, mirrors, rel_emb,
         query_rel, rel_score,
     )
-    h_out, loss, aggregate, pre_grad, agg_tiles = middle(
+    h_out, loss, agg_all, pre_all, agg_tiles = middle(
+        partial_low,
         partial,
         self_part,
         w_in,
         query_part,
         query_head.reshape(1, -1),
         true_tail.reshape(1, -1),
-        allowed,
+        allowed.T,
     )
     tiles, rel_part = backward(
         adj_source, adj_target, adj_relation, live_blocks, adj_values, agg_tiles
@@ -873,9 +947,9 @@
     node_grad, rel_grad, w_in_grad, w_self_grad = give_back(
         tiles.reshape(2, 8, 4, 128, 256),
         rel_part,
-        aggregate,
-        pre_grad,
-        node_emb,
+        agg_all,
+        pre_all,
+        node_tiles,
         w_self,
         requests,
         rel_emb.shape[0],

time: 293 us -> 240 us (0.82)
  Pallas kernels: 282 us -> 230 us
    pallas_call x2, Pallas kernels: 191 us -> 135 us  [the longest x1 71.9 us: middle(): pl.pallas_call(middle_kernel, name='middle', out_shape=(jax.ShapeDtypeStr...]
    unnamed x15 -> x12, local copies, waits for them, and re-layouts: 9 us -> 7.99 us
where the time goes in v2:
time: 240 us; the launch traced here: 239 us
  Pallas kernels  230 us (96%)
  local copies, waits for them, and re-layouts  7.99 us (3%)
    pallas_call x1, Pallas kernels, middle(): pl.pallas_call(middle_kernel, name='middle', out_shape=(jax.ShapeDtypeStr...  71.9 us
    pallas_call x1, Pallas kernels, give_back(): pl.pallas_call(functools.partial(return_kernel, len(ar)), name='give_back...  63.6 us
    pallas_call x1, Pallas kernels, fetch(): pl.pallas_call(fetch_kernel, name='fetch', out_shape=(jax.ShapeDtypeStruc...  50.7 us
    pallas_call x1, Pallas kernels, forward(): pl.pallas_call(forward_kernel, name='forward_blocks', grid=(blocks // GRO...  21.9 us
    pallas_call x1, Pallas kernels, backward(): pl.pallas_call(backward_kernel, name='backward_blocks', grid=(blocks // G...  21.8 us
    unnamed x12, local copies, waits for them, and re-layouts  7.99 us

profile of v2, /device:TPU:1, one launch (start us, length us, event | category | flops | bytes accessed | tf_op | source)
XLA Modules:
  0.0 239.2 jit_solution(3593706351493937671)
XLA Ops:
  1.3 50.7 %fetch.1 = (bf16[2,8,4,128,256]{4,3,2,1,0:T(8,128)(2,1)}, s32[16,1,128]{2,1,0:T(1,128)}, f32[128,512]{1,0:T(8,128)}) custom-call(bf16[4,128,512]{2,1,0:T(8,128)(2,1)} %bitcast.10, s32[1,32]{1,0:T(1,128)} %bitcast.16, bf16[512,512]{1,0:T(8,128)(2,1)} %w_self.3), custom_call_target="tpu_custom_call" | custom-call | tf_op jit(solution)/shard_map/fetch/pallas_call | solution.py:283
  52.0 21.9 %forward_blocks.1 = (f32[4,128,512]{2,1,0:T(8,128)}, bf16[4,128,512]{2,1,0:T(8,128)(2,1)}, f32[128,512]{1,0:T(8,128)}) custom-call(s32[1,1,192]{2,1,0:T(1,128)} %source.3, s32[1,1,192]{2,1,0:T(1,128)} %target.3, s32[1,1,192]{2,1,0:T(1,128)} %relation.3, s32[1,1]{1,0:T(1,128)S(6)} %copy.27.live, bf16[1,1,192,128,128]{4,3,2,1,0:T(8,128)(2,1)} %values.3, ...), custom_call_target="tpu_custom_call" | custom-call | tf_op jit(solution)/shard_map/forward_blocks/pallas_call | solution.py:367
  73.9 71.9 %middle.1 = (bf16[1,128,512]{2,1,0:T(8,128)(2,1)}, f32[8,1,128]{2,1,0:T(1,128)}, bf16[4,128,512]{2,1,0:T(8,128)(2,1)}, bf16[4,128,512]{2,1,0:T(8,128)(2,1)}, bf16[4,128,512]{2,1,0:T(8,128)(2,1)}) custom-call(bf16[4,128,512]{2,1,0:T(8,128)(2,1)} %get-tuple-element.24.partial_low, f32[4,128,512]{2,1,0:T(8,128)} %get-tuple-element.25.partial, ...), custom_call_target="tpu_custom_call" | custom-call | tf_op jit(solution)/shard_map/middle/pallas_call | solution.py:677
  145.8 21.8 %backward_blocks.1 = (bf16[2,32,128,256]{3,2,1,0:T(8,128)(2,1)}, f32[256,512]{1,0:T(8,128)}) custom-call(s32[1,1,192]{2,1,0:T(1,128)} %source.3, s32[1,1,192]{2,1,0:T(1,128)} %target.3, s32[1,1,192]{2,1,0:T(1,128)} %relation.3, s32[1,1]{1,0:T(1,128)S(6)} %copy.27.live, bf16[1,1,192,128,128]{4,3,2,1,0:T(8,128)(2,1)} %values.3, ...), custom_call_target="tpu_custom_call" | custom-call | tf_op jit(solution)/shard_map/backward_blocks/pallas_call | solution.py:425
  167.6 0.0 copy-start.1
  167.6 0.0 copy-start.2
  167.6 63.6 %give_back.1 = (f32[1,128,512]{2,1,0:T(8,128)}, f32[225,512]{1,0:T(8,128)}, f32[512,512]{1,0:T(8,128)}, f32[512,512]{1,0:T(8,128)}) custom-call(bf16[2,8,4,128,256]{4,3,2,1,0:T(8,128)(2,1)} %bitcast.8, f32[256,512]{1,0:T(8,128)} %get-tuple-element.32.rel_part, bf16[4,128,512]{2,1,0:T(8,128)(2,1)} %get-tuple-element.33.agg_all, ...), custom_call_target="tpu_custom_call" | custom-call | tf_op jit(solution)/shard_map/give_back/pallas_call | solution.py:879
  231.2 0.0 copy-start
  231.2 0.0 copy-done.1
  231.2 0.7 copy.28
  231.9 0.0 copy-done.2
  231.9 0.6 copy.29
  232.5 1.7 copy.30
  234.2 1.8 copy.31
  236.0 2.3 copy.32
  238.2 0.0 copy-done
  238.2 1.0 copy.33
Async XLA Ops:
  167.6 63.6 %copy-start.1 = (bf16[1,128,512]{2,1,0:T(8,128)(2,1)S(1)}, bf16[1,128,512]{2,1,0:T(8,128)(2,1)}, u32[]{:S(2)}) copy-start(bf16[1,128,512]{2,1,0:T(8,128)(2,1)} %get-tuple-element.46) | copy-start | bytes 393220
  167.6 64.3 %copy-start.2 = (f32[8,1,128]{2,1,0:T(1,128)S(1)}, f32[8,1,128]{2,1,0:T(1,128)}, u32[]{:S(2)}) copy-start(f32[8,1,128]{2,1,0:T(1,128)} %get-tuple-element.29) | copy-start | bytes 12292
  231.2 7.0 %copy-start = (f32[512,512]{1,0:T(8,128)S(1)}, f32[512,512]{1,0:T(8,128)}, u32[]{:S(2)}) copy-start(f32[512,512]{1,0:T(8,128)} %get-tuple-element.51) | copy-start | bytes 3145732

commit v3 on v2

--- a/solution.py
+++ b/solution.py
@@ -116,7 +116,6 @@
         shapes = [
             pltpu.VMEM((4, shards, height, 128), BF),
             pltpu.VMEM((2, shards, height, 128), BF),
-            pltpu.VMEM((4, shards, height, 128), BF),
         ]
         for level in range(depth):
             shapes.append(pltpu.VMEM((2, shards // 4**level, height, 128), BF))
@@ -305,7 +304,7 @@
     )(node_tiles, wanted, w_self)
 
 
-GROUP = 8
+GROUP = 24
 
 
 def slots_of(source):
@@ -321,11 +320,9 @@
     step = pl.program_id(0)
     first = (lax.axis_index("grp") * 2 + lax.axis_index("cand") % 2) * 128
 
-    @pl.when(step < 16)
-    def _():
-        for j in range(8):
-            row = step * 8 + j
-            query_part[pl.ds(row, 1), :] = rel_score[pl.ds(query_rel[first + row], 1), :]
+    for j in range(16):
+        row = step * 16 + j
+        query_part[pl.ds(row, 1), :] = rel_score[pl.ds(query_rel[first + row], 1), :]
 
     @pl.when(step == 0)
     def _():
@@ -382,7 +379,10 @@
     )
 
 
-def backward_kernel(source, target, relation, live, values, agg, tiles_out, rel_out, tiles):
+def backward_kernel(
+    source, target, relation, live, values, agg, h_in, loss_in,
+    tiles_out, rel_out, h_out, loss_out, tiles,
+):
     step = pl.program_id(0)
 
     @pl.when(step == 0)
@@ -394,6 +394,9 @@
 
         lax.fori_loop(0, 32, clear, 0)
         rel_out[...] = jnp.zeros_like(rel_out)
+        h_out[...] = h_in[...]
+        for j in range(8):
+            loss_out[j : j + 1, :] = loss_in[j]
 
     count = live[0, 0]
 
@@ -420,7 +423,7 @@
         lax.fori_loop(0, 32, store, 0)
 
 
-def backward(adj_source, adj_target, adj_relation, live_blocks, adj_values, agg_tiles):
+def backward(adj_source, adj_target, adj_relation, live_blocks, adj_values, agg_tiles, h, loss):
     blocks = adj_values.shape[2]
     return pl.pallas_call(
         backward_kernel,
@@ -429,12 +432,14 @@
         out_shape=(
             jax.ShapeDtypeStruct((2, 32, 128, 256), BF),
             jax.ShapeDtypeStruct((256, 512), F32),
+            jax.ShapeDtypeStruct(h.shape, h.dtype),
+            jax.ShapeDtypeStruct((8, 128), F32),
         ),
-        in_specs=adjacency_specs(blocks) + [VMEM_SPEC],
-        out_specs=(VMEM_SPEC, VMEM_SPEC),
+        in_specs=adjacency_specs(blocks) + [VMEM_SPEC] * 3,
+        out_specs=(VMEM_SPEC,) * 4,
         scratch_shapes=[pltpu.VMEM((2, 32, 128, 256), F32)],
         compiler_params=pltpu.CompilerParams(vmem_limit_bytes=LIMIT),
-    )(adj_source, adj_target, adj_relation, live_blocks, adj_values, agg_tiles)
+    )(adj_source, adj_target, adj_relation, live_blocks, adj_values, agg_tiles, h, loss)
 
 
 def exchange_sum(me, wire, send, recv, out, during=None):
@@ -719,10 +724,11 @@
 def return_kernel(
     n_ar,
     tiles, rel_part, agg_all, pre_all, node, w_self, requests,
-    node_grad, rel_grad, w_in_grad, w_self_grad,
-    arrived, shipped, joined, own_sum, y_send, y_recv, self_grad, w_all, *rest,
+    node_grad, summed, w_all,
+    arrived, shipped, joined, own_sum, y_send, y_recv, self_grad, *rest,
 ):
-    ar_refs = rest[:n_ar]
+    ar_refs = list(rest[:n_ar])
+    ar_refs.insert(2, summed)
     send_sem, recv_sem, local_sem = rest[n_ar:]
     me = Place()
     devices = []
@@ -857,22 +863,12 @@
         other = (me.g + 4 - d) % 4
         w_rows.append(wire.put(w_all.at[other, pair], w_all.at[other, pair], me.sibling()))
     both.wait_recv()
-    for j in range(4):
-        whole = reduce.out[j, :, 16:32].astype(F32).reshape(256, 128)
-        rel_grad[:, 128 * j : 128 * j + 128] = whole[: rel_grad.shape[0]]
     for copy in w_rows:
         copy.wait_recv()
-    for j in range(4):
-        for q in range(2):
-            rows = slice(256 * q, 256 * q + 256)
-            for at, target in ((q, w_in_grad), (2 + q, w_self_grad)):
-                target[rows, 128 * j : 128 * j + 128] = (
-                    w_all[j, at].astype(F32).reshape(256, 128)
-                )
     wire.drain()
 
 
-def give_back(tiles, rel_part, agg_all, pre_all, node_tiles, w_self, requests, relations):
+def give_back(tiles, rel_part, agg_all, pre_all, node_tiles, w_self, requests):
     depth = w_self.shape[0]
     ar = AllReduce.scratch(16, STAGES_CAND, 32)
     copies = 56 + 6 + 6 + (1 + 12 + 12) + 1 + 3 + 4
@@ -881,12 +877,11 @@
         name="give_back",
         out_shape=(
             jax.ShapeDtypeStruct((1, 128, depth), F32),
-            jax.ShapeDtypeStruct((relations, depth), F32),
-            jax.ShapeDtypeStruct((depth, depth), F32),
-            jax.ShapeDtypeStruct((depth, depth), F32),
+            jax.ShapeDtypeStruct((4, 16, 32, 128), BF),
+            jax.ShapeDtypeStruct((4, 4, 16, 16, 128), BF),
         ),
         in_specs=[ANY_SPEC] + [VMEM_SPEC] * 5 + [SMEM_SPEC],
-        out_specs=(VMEM_SPEC,) * 4,
+        out_specs=(VMEM_SPEC,) * 3,
         scratch_shapes=[
             pltpu.VMEM((2, 8, 4, 128, 256), BF),
             pltpu.VMEM((2, 3, 4, 128, 256), BF),
@@ -895,7 +890,6 @@
             pltpu.VMEM((2, 3, 128, 256), BF),
             pltpu.VMEM((2, 3, 128, 256), BF),
             pltpu.VMEM((128, depth), F32),
-            pltpu.VMEM((4, 4, 16, 16, 128), BF),
             *ar,
             pltpu.SemaphoreType.DMA((copies,)),
             pltpu.SemaphoreType.DMA((copies,)),
@@ -905,6 +899,34 @@
             collective_id=2, has_side_effects=True, vmem_limit_bytes=LIMIT
         ),
     )(tiles, rel_part, agg_all, pre_all, node_tiles, w_self, requests)
+
+
+def finish_kernel(node_in, summed, w_all, node_grad, rel_grad, w_in_grad, w_self_grad):
+    node_grad[...] = node_in[...]
+    for j in range(4):
+        cols = slice(128 * j, 128 * j + 128)
+        whole = summed[j, :, 16:32].astype(F32).reshape(256, 128)
+        rel_grad[:, cols] = whole[: rel_grad.shape[0]]
+        for q in range(2):
+            rows = slice(256 * q, 256 * q + 256)
+            for at, target in ((q, w_in_grad), (2 + q, w_self_grad)):
+                target[rows, cols] = w_all[j, at].astype(F32).reshape(256, 128)
+
+
+def finish(node_grad, summed, w_all, relations):
+    depth = node_grad.shape[2]
+    return pl.pallas_call(
+        finish_kernel,
+        name="finish",
+        out_shape=(
+            jax.ShapeDtypeStruct(node_grad.shape, F32),
+            jax.ShapeDtypeStruct((relations, depth), F32),
+            jax.ShapeDtypeStruct((depth, depth), F32),
+            jax.ShapeDtypeStruct((depth, depth), F32),
+        ),
+        in_specs=[VMEM_SPEC] * 3,
+        out_specs=(VMEM_SPEC,) * 4,
+    )(node_grad, summed, w_all)
 
 
 def body(
@@ -931,7 +953,7 @@
         adj_source, adj_target, adj_relation, live_blocks, adj_values, mirrors, rel_emb,
         query_rel, rel_score,
     )
-    h_out, loss, agg_all, pre_all, agg_tiles = middle(
+    h, loss, agg_all, pre_all, agg_tiles = middle(
         partial_low,
         partial,
         self_part,
@@ -941,10 +963,10 @@
         true_tail.reshape(1, -1),
         allowed.T,
     )
-    tiles, rel_part = backward(
-        adj_source, adj_target, adj_relation, live_blocks, adj_values, agg_tiles
+    tiles, rel_part, h_out, loss = backward(
+        adj_source, adj_target, adj_relation, live_blocks, adj_values, agg_tiles, h, loss
     )
-    node_grad, rel_grad, w_in_grad, w_self_grad = give_back(
+    node_grad, summed, w_all = give_back(
         tiles.reshape(2, 8, 4, 128, 256),
         rel_part,
         agg_all,
@@ -952,7 +974,9 @@
         node_tiles,
         w_self,
         requests,
-        rel_emb.shape[0],
+    )
+    node_grad, rel_grad, w_in_grad, w_self_grad = finish(
+        node_grad, summed, w_all, rel_emb.shape[0]
     )
     return (h_out, loss.reshape(-1), node_grad, rel_grad, w_in_grad, w_self_grad)
 

time: 240 us -> 218 us (0.908)
  Pallas kernels: 230 us -> 217 us
  local copies, waits for them, and re-layouts: 7.99 us -> 0 us
    pallas_call x1, Pallas kernels: 21.9 us -> 12.4 us  [forward(): pl.pallas_call(forward_kernel, name='forward_blocks', grid=(blocks // GRO...]
    pallas_call x1, Pallas kernels: 21.8 us -> 12.5 us  [backward(): pl.pallas_call(backward_kernel, name='backward_blocks', grid=(blocks // G...]
    unnamed x12 -> x0, local copies, waits for them, and re-layouts: 7.99 us -> none
    pallas_call x0 -> x1, Pallas kernels: none -> 3.12 us  [finish(): pl.pallas_call(finish_kernel, name='finish', out_shape=(jax.ShapeDtypeStr...]
where the time goes in v3:
time: 218 us
  Pallas kernels  217 us (100%)
    pallas_call x1, Pallas kernels, middle(): pl.pallas_call(middle_kernel, name='middle', out_shape=(jax.ShapeDtypeStr...  72.9 us
    pallas_call x1, Pallas kernels, give_back(): pl.pallas_call(functools.partial(return_kernel, len(ar)), name='give_back...  65.1 us
    pallas_call x1, Pallas kernels, fetch(): pl.pallas_call(fetch_kernel, name='fetch', out_shape=(jax.ShapeDtypeStruc...  50.7 us
    pallas_call x1, Pallas kernels, backward(): pl.pallas_call(backward_kernel, name='backward_blocks', grid=(blocks // G...  12.5 us
    pallas_call x1, Pallas kernels, forward(): pl.pallas_call(forward_kernel, name='forward_blocks', grid=(blocks // GRO...  12.4 us

profile of v3, /device:TPU:1, one launch (start us, length us, event | category | flops | bytes accessed | tf_op | source)
XLA Modules:
  0.0 218.1 jit_solution(13205728290483508124)
XLA Ops:
  1.3 50.7 %fetch.1 = (bf16[2,8,4,128,256]{4,3,2,1,0:T(8,128)(2,1)}, s32[16,1,128]{2,1,0:T(1,128)}, f32[128,512]{1,0:T(8,128)}) custom-call(bf16[4,128,512]{2,1,0:T(8,128)(2,1)} %bitcast.10, s32[1,32]{1,0:T(1,128)} %bitcast.15, bf16[512,512]{1,0:T(8,128)(2,1)} %w_self.3), custom_call_target="tpu_custom_call" | custom-call | tf_op jit(solution)/shard_map/fetch/pallas_call | solution.py:282
  52.0 12.4 %forward_blocks.1 = (f32[4,128,512]{2,1,0:T(8,128)}, bf16[4,128,512]{2,1,0:T(8,128)(2,1)}, f32[128,512]{1,0:T(8,128)}) custom-call(s32[1,1,192]{2,1,0:T(1,128)} %source.3, s32[1,1,192]{2,1,0:T(1,128)} %target.3, s32[1,1,192]{2,1,0:T(1,128)} %relation.3, s32[1,1]{1,0:T(1,128)S(6)} %copy.21.live, bf16[1,1,192,128,128]{4,3,2,1,0:T(8,128)(2,1)} %values.3, ...), custom_call_target="tpu_custom_call" | custom-call | tf_op jit(solution)/shard_map/forward_blocks/pallas_call | solution.py:364
  64.4 72.9 %middle.1 = (bf16[1,128,512]{2,1,0:T(8,128)(2,1)}, f32[8,1,128]{2,1,0:T(1,128)}, bf16[4,128,512]{2,1,0:T(8,128)(2,1)}, bf16[4,128,512]{2,1,0:T(8,128)(2,1)}, bf16[4,128,512]{2,1,0:T(8,128)(2,1)}) custom-call(bf16[4,128,512]{2,1,0:T(8,128)(2,1)} %get-tuple-element.29.partial_low, f32[4,128,512]{2,1,0:T(8,128)} %get-tuple-element.30.partial, ...), custom_call_target="tpu_custom_call" | custom-call | tf_op jit(solution)/shard_map/middle/pallas_call | solution.py:682
  137.3 12.5 %backward_blocks.1 = (bf16[2,32,128,256]{3,2,1,0:T(8,128)(2,1)}, f32[256,512]{1,0:T(8,128)}, bf16[1,128,512]{2,1,0:T(8,128)(2,1)}, f32[8,128]{1,0:T(8,128)}) custom-call(s32[1,1,192]{2,1,0:T(1,128)} %source.3, s32[1,1,192]{2,1,0:T(1,128)} %target.3, s32[1,1,192]{2,1,0:T(1,128)} %relation.3, s32[1,1]{1,0:T(1,128)S(6)} %copy.21.live, ...), custom_call_target="tpu_custom_call" | custom-call | tf_op jit(solution)/shard_map/backward_blocks/pallas_call | solution.py:428
  149.8 65.1 %give_back.1 = (f32[1,128,512]{2,1,0:T(8,128)}, bf16[4,16,32,128]{3,2,1,0:T(8,128)(2,1)}, bf16[4,4,16,16,128]{4,3,2,1,0:T(8,128)(2,1)}) custom-call(bf16[2,8,4,128,256]{4,3,2,1,0:T(8,128)(2,1)} %bitcast.8, f32[256,512]{1,0:T(8,128)} %get-tuple-element.39.rel_part, bf16[4,128,512]{2,1,0:T(8,128)(2,1)} %get-tuple-element.40.agg_all, ...), custom_call_target="tpu_custom_call" | custom-call | tf_op jit(solution)/shard_map/give_back/pallas_call | solution.py:875
  214.9 3.1 %finish.1 = (f32[1,128,512]{2,1,0:T(8,128)}, f32[225,512]{1,0:T(8,128)}, f32[512,512]{1,0:T(8,128)}, f32[512,512]{1,0:T(8,128)}) custom-call(f32[1,128,512]{2,1,0:T(8,128)} %get-tuple-element.43.node_in, bf16[4,16,32,128]{3,2,1,0:T(8,128)(2,1)} %get-tuple-element.44.summed, bf16[4,4,16,16,128]{4,3,2,1,0:T(8,128)(2,1)} %get-tuple-element.45.w_all), custom_call_target="tpu_custom_call" | custom-call | tf_op jit(solution)/shard_map/finish/pallas_call | solution.py:918

commit v4 on v3

--- a/solution.py
+++ b/solution.py
@@ -122,12 +122,13 @@
             shapes.append(pltpu.VMEM((2, 3, shards // 4 ** (level + 1), height, 128), BF))
         return shapes
 
-    def __init__(self, me, wire, shards, stages, refs):
+    def __init__(self, me, wire, shards, stages, refs, summed, w_all):
         self.me, self.wire, self.shards, self.stages = me, wire, shards, stages
-        self.part, self.rcore, self.out = refs[:3]
+        self.part, self.rcore = refs[:2]
+        self.summed, self.w_all = summed, w_all
         depth = len(stages[0])
-        self.acc = refs[3 : 3 + 2 * depth : 2]
-        self.recv = refs[4 : 4 + 2 * depth : 2]
+        self.acc = refs[2 : 2 + 2 * depth : 2]
+        self.recv = refs[3 : 3 + 2 * depth : 2]
         self.sizes = [shards // 4 ** (i + 1) for i in range(depth)]
 
     def steps(self):
@@ -180,12 +181,21 @@
                     if level + 1 < depth:
                         self.acc[level + 1][col, at] = value.astype(BF)
                     else:
-                        self.out[mine + col, pl.ds(offsets[col] + at.start, at.size)] = (
-                            value.astype(BF)
-                        )
+                        final = value.astype(BF)
+                        place = pl.ds(offsets[col] + at.start, at.size)
+                        self.w_all[me.g, mine + col, place] = final[:, 0:16]
+                        self.summed[mine + col, place] = final[:, 16:32]
 
                 add_up(terms, write, size)
             history.append(tuple(offsets))
+        copies = []
+        for d in (1, 3, 2):
+            for col in range(2):
+                place = self.w_all.at[me.g, mine + col, pl.ds(offsets[col], self.sizes[-1])]
+                copies.append(wire.put(place, place, me.peer("y", (me.g + d) % 4)))
+        yield
+        for copy in copies:
+            copy.wait_recv()
         for level in reversed(range(depth)):
             size = self.sizes[level]
             copies = []
@@ -193,8 +203,12 @@
                 for col in range(2):
                     axis = self.stages[col][level]
                     other = (me.at(axis) + d) % 4
-                    place = self.out.at[mine + col, pl.ds(history[level][col], size)]
-                    copies.append(wire.put(place, place, me.peer(axis, other)))
+                    shards = pl.ds(history[level][col], size)
+                    for place in (
+                        self.summed.at[mine + col, shards],
+                        self.w_all.at[:, mine + col, shards],
+                    ):
+                        copies.append(wire.put(place, place, me.peer(axis, other)))
             yield
             for copy in copies:
                 copy.wait_recv()
@@ -211,9 +225,9 @@
         devices.append(me.dev(me.g, me.x * 8 + (me.zk + e) % 8))
     for e in range(1, 8):
         other = (me.xk + e) % 8
-        if e == 7:
-            pass
         devices.append(me.dev(me.g, (other // 2) * 8 + me.z * 2 + other % 2))
+    for d in (1, 2, 3):
+        devices.append(me.peer("y", (me.g + d) % 4))
     enter(devices)
     wire = Wire(send_sem, recv_sem)
     wanted_row[...] = jnp.zeros_like(wanted_row)
@@ -224,7 +238,9 @@
         for col, axis in ((0, "x"), (1, "z")):
             other = (me.at(axis) + d) % 4
             first[col, d] = wire.put(
-                node.at[:, :, halves[col]], gathered[3 * col + d - 1], me.peer(axis, other)
+                node.at[me.g, :, halves[col]],
+                gathered[3 * col + d - 1].at[me.g],
+                me.peer(axis, other),
             )
     asks = []
     for e in range(1, 8):
@@ -238,6 +254,17 @@
             )
     requests[me.zk] = wanted_row[...]
     requests[8 + me.xk] = wanted_row[...]
+    spread = {}
+
+    def pass_on(d):
+        for col in range(2):
+            first[col, d].wait_recv()
+            place = gathered[3 * col + d - 1].at[me.g]
+            spread[col, d] = [
+                wire.put(place, place, me.peer("y", (me.g + e) % 4)) for e in (1, 3, 2)
+            ]
+
+    pass_on(1)
     for copy in asks:
         copy.wait_recv()
     local = pltpu.make_async_copy(requests, request_s, local_sem)
@@ -247,7 +274,8 @@
     for d in (0, 1, 3, 2):
         for col, axis in ((0, "x"), (1, "z")):
             if d:
-                first[col, d].wait_recv()
+                for copy in spread[col, d]:
+                    copy.wait_recv()
             origin = (me.at(axis) + 4 - d) % 4
             own_slot = me.zk if col == 0 else me.xk
             owner = origin * 8 + me.zk if col == 0 else me.x * 8 + origin * 2 + me.k
@@ -269,7 +297,9 @@
                             devices[7 * col + e - 1],
                         )
                     )
-
+        if d == 0:
+            pass_on(3)
+            pass_on(2)
     self_part[...] = dot(node[me.g], w_self[...])
     for copy in moved:
         copy.wait_recv()
@@ -278,7 +308,7 @@
 
 def fetch(node_tiles, wanted, w_self):
     depth = node_tiles.shape[2]
-    copies = 6 + 14 + 56
+    copies = 6 + 14 + 56 + 18
     return pl.pallas_call(
         fetch_kernel,
         name="fetch",
@@ -725,10 +755,9 @@
     n_ar,
     tiles, rel_part, agg_all, pre_all, node, w_self, requests,
     node_grad, summed, w_all,
-    arrived, shipped, joined, own_sum, y_send, y_recv, self_grad, *rest,
+    arrived, shipped, y_recv, x_send, joined, self_grad, *rest,
 ):
-    ar_refs = list(rest[:n_ar])
-    ar_refs.insert(2, summed)
+    ar_refs = rest[:n_ar]
     send_sem, recv_sem, local_sem = rest[n_ar:]
     me = Place()
     devices = []
@@ -741,7 +770,7 @@
         devices.append(me.peer("y", (me.g + d) % 4))
     enter(devices)
     wire = Wire(send_sem, recv_sem)
-    reduce = AllReduce(me, wire, 16, STAGES_CAND, ar_refs)
+    reduce = AllReduce(me, wire, 16, STAGES_CAND, ar_refs, summed, w_all)
     steps = reduce.steps()
 
     def advance():
@@ -764,7 +793,6 @@
                 )
 
     send_round(order[0])
-    send_round(order[1])
     local = []
     for col in range(2):
         copy = pltpu.make_async_copy(
@@ -788,14 +816,34 @@
                 .astype(BF)
             )
     advance()
+    send_round(order[1])
     self_grad[...] = dot(pre_all[me.g], w_self[...], NT)
     advance()
     for copy in local:
         copy.wait()
+    over_y = {}
     second = []
+
+    def combine(d, col):
+        for copy in over_y[d, col]:
+            copy.wait_recv()
+        total = shipped[col, d, me.g].astype(F32)
+        for m in range(3):
+            total = total + y_recv[col, d, m].astype(F32)
+        return total
+
+    def send_combined(d):
+        for col, axis in axes:
+            x_send[col, d - 1] = combine(d, col).astype(BF)
+            second.append(
+                wire.put(
+                    x_send.at[col, d - 1],
+                    joined.at[col, d - 1],
+                    me.peer(axis, (me.at(axis) + d) % 4),
+                )
+            )
+
     for at, d in enumerate(order):
-        if at + 2 < 4:
-            send_round(order[at + 2])
         for col, axis in axes:
             place = (me.at(axis) + d) % 4
             owner = place * 8 + me.zk if col == 0 else me.x * 8 + place * 2 + me.k
@@ -809,61 +857,36 @@
                     total = jnp.zeros((32, 256), F32)
                     for m in range(8):
                         total = total + jnp.where(index[m] == s, values[m], 0.0)
-                    if d == 0:
-                        own_sum[col, s, rows, :] = total
-                    else:
-                        shipped[col, d - 1, s, rows, :] = total.astype(BF)
-            if d:
-                second.append(
+                    shipped[col, d, s, rows, :] = total.astype(BF)
+            over_y[d, col] = []
+            for e in (1, 3, 2):
+                s = (me.g + e) % 4
+                over_y[d, col].append(
                     wire.put(
-                        shipped.at[col, d - 1], joined.at[col, d - 1], me.peer(axis, place)
+                        shipped.at[col, d, s], y_recv.at[col, d, e - 1], me.peer("y", s)
                     )
                 )
         advance()
+        if at + 2 < 4:
+            send_round(order[at + 2])
+        if at:
+            send_combined(order[at - 1])
+    advance()
+    pair = pl.ds(2 * me.k, 2)
+    last = [
+        wire.put(summed.at[pair], summed.at[pair], me.sibling()),
+        wire.put(w_all.at[:, pair], w_all.at[:, pair], me.sibling()),
+    ]
     for copy in second:
         copy.wait_recv()
-    third = []
-    for d in (1, 3, 2, 0):
-        s = (me.g + d) % 4
-        for col in range(2):
-            total = own_sum[col, s]
-            for m in range(3):
-                total = total + joined[col, m, s].astype(F32)
-            if d == 0:
-                own_sum[col, s] = total
-            else:
-                y_send[col, d - 1] = total.astype(BF)
-                third.append(
-                    wire.put(y_send.at[col, d - 1], y_recv.at[col, d - 1], me.peer("y", s))
-                )
-    advance()
-    advance()
-    mine = 2 * me.k
-    pair = pl.ds(mine, 2)
-    both = wire.put(reduce.out.at[pair], reduce.out.at[pair], me.sibling())
     for col in range(2):
-        w_all[me.g, mine + col] = reduce.out[mine + col, :, 0:16]
-    w_copies = {}
-    for d in (1, 3, 2):
-        w_copies[d] = wire.put(
-            w_all.at[me.g, pair], w_all.at[me.g, pair], me.peer("y", (me.g + d) % 4)
-        )
-    w_rows = [wire.put(w_all.at[me.g, pair], w_all.at[me.g, pair], me.sibling())]
-    for copy in third:
-        copy.wait_recv()
-    for col in range(2):
-        total = own_sum[col, me.g]
+        total = combine(0, col)
         for m in range(3):
-            total = total + y_recv[col, m].astype(F32)
+            total = total + joined[col, m].astype(F32)
         node_grad[0, :, 256 * col : 256 * col + 256] = (
             total + self_grad[:, 256 * col : 256 * col + 256]
         )
-    for d in (1, 3, 2):
-        w_copies[d].wait_recv()
-        other = (me.g + 4 - d) % 4
-        w_rows.append(wire.put(w_all.at[other, pair], w_all.at[other, pair], me.sibling()))
-    both.wait_recv()
-    for copy in w_rows:
+    for copy in last:
         copy.wait_recv()
     wire.drain()
 
@@ -871,22 +894,21 @@
 def give_back(tiles, rel_part, agg_all, pre_all, node_tiles, w_self, requests):
     depth = w_self.shape[0]
     ar = AllReduce.scratch(16, STAGES_CAND, 32)
-    copies = 56 + 6 + 6 + (1 + 12 + 12) + 1 + 3 + 4
+    copies = 56 + 24 + 6 + (1 + 12 + 6 + 24) + 2
     return pl.pallas_call(
         functools.partial(return_kernel, len(ar)),
         name="give_back",
         out_shape=(
             jax.ShapeDtypeStruct((1, 128, depth), F32),
-            jax.ShapeDtypeStruct((4, 16, 32, 128), BF),
+            jax.ShapeDtypeStruct((4, 16, 16, 128), BF),
             jax.ShapeDtypeStruct((4, 4, 16, 16, 128), BF),
         ),
         in_specs=[ANY_SPEC] + [VMEM_SPEC] * 5 + [SMEM_SPEC],
         out_specs=(VMEM_SPEC,) * 3,
         scratch_shapes=[
             pltpu.VMEM((2, 8, 4, 128, 256), BF),
-            pltpu.VMEM((2, 3, 4, 128, 256), BF),
-            pltpu.VMEM((2, 3, 4, 128, 256), BF),
-            pltpu.VMEM((2, 4, 128, 256), F32),
+            pltpu.VMEM((2, 4, 4, 128, 256), BF),
+            pltpu.VMEM((2, 4, 3, 128, 256), BF),
             pltpu.VMEM((2, 3, 128, 256), BF),
             pltpu.VMEM((2, 3, 128, 256), BF),
             pltpu.VMEM((128, depth), F32),
@@ -905,7 +927,7 @@
     node_grad[...] = node_in[...]
     for j in range(4):
         cols = slice(128 * j, 128 * j + 128)
-        whole = summed[j, :, 16:32].astype(F32).reshape(256, 128)
+        whole = summed[j].astype(F32).reshape(256, 128)
         rel_grad[:, cols] = whole[: rel_grad.shape[0]]
         for q in range(2):
             rows = slice(256 * q, 256 * q + 256)

time: 218 us -> 195 us (0.89)
  Pallas kernels: 217 us -> 193 us
    pallas_call x1, Pallas kernels: 65.1 us -> 48.8 us  [give_back(): pl.pallas_call(functools.partial(return_kernel, len(ar)), name='give_back...]
    pallas_call x1, Pallas kernels: 50.7 us -> 43.7 us  [fetch(): pl.pallas_call(fetch_kernel, name='fetch', out_shape=(jax.ShapeDtypeStruc...]
where the time goes in v4:
time: 195 us
  Pallas kernels  193 us (99%)
    pallas_call x1, Pallas kernels, middle(): pl.pallas_call(middle_kernel, name='middle', out_shape=(jax.ShapeDtypeStr...  70.8 us
    pallas_call x1, Pallas kernels, give_back(): pl.pallas_call(functools.partial(return_kernel, len(ar)), name='give_back...  48.8 us
    pallas_call x1, Pallas kernels, fetch(): pl.pallas_call(fetch_kernel, name='fetch', out_shape=(jax.ShapeDtypeStruc...  43.7 us
    pallas_call x1, Pallas kernels, backward(): pl.pallas_call(backward_kernel, name='backward_blocks', grid=(blocks // G...  13.5 us
    pallas_call x1, Pallas kernels, forward(): pl.pallas_call(forward_kernel, name='forward_blocks', grid=(blocks // GRO...  13.5 us

profile of v4, /device:TPU:1, one launch (start us, length us, event | category | flops | bytes accessed | tf_op | source)
XLA Modules:
  0.0 194.6 jit_solution(17126795795623298520)
XLA Ops:
  1.3 43.7 %fetch.1 = (bf16[2,8,4,128,256]{4,3,2,1,0:T(8,128)(2,1)}, s32[16,1,128]{2,1,0:T(1,128)}, f32[128,512]{1,0:T(8,128)}) custom-call(bf16[4,128,512]{2,1,0:T(8,128)(2,1)} %bitcast.10, s32[1,32]{1,0:T(1,128)} %bitcast.15, bf16[512,512]{1,0:T(8,128)(2,1)} %w_self.3), custom_call_target="tpu_custom_call" | custom-call | tf_op jit(solution)/shard_map/fetch/pallas_call | solution.py:312
  45.0 13.5 %forward_blocks.1 = (f32[4,128,512]{2,1,0:T(8,128)}, bf16[4,128,512]{2,1,0:T(8,128)(2,1)}, f32[128,512]{1,0:T(8,128)}) custom-call(s32[1,1,192]{2,1,0:T(1,128)} %source.3, s32[1,1,192]{2,1,0:T(1,128)} %target.3, s32[1,1,192]{2,1,0:T(1,128)} %relation.3, s32[1,1]{1,0:T(1,128)S(6)} %copy.21.live, bf16[1,1,192,128,128]{4,3,2,1,0:T(8,128)(2,1)} %values.3, ...), custom_call_target="tpu_custom_call" | custom-call | tf_op jit(solution)/shard_map/forward_blocks/pallas_call | solution.py:394
  58.5 70.8 %middle.1 = (bf16[1,128,512]{2,1,0:T(8,128)(2,1)}, f32[8,1,128]{2,1,0:T(1,128)}, bf16[4,128,512]{2,1,0:T(8,128)(2,1)}, bf16[4,128,512]{2,1,0:T(8,128)(2,1)}, bf16[4,128,512]{2,1,0:T(8,128)(2,1)}) custom-call(bf16[4,128,512]{2,1,0:T(8,128)(2,1)} %get-tuple-element.29.partial_low, f32[4,128,512]{2,1,0:T(8,128)} %get-tuple-element.30.partial, ...), custom_call_target="tpu_custom_call" | custom-call | tf_op jit(solution)/shard_map/middle/pallas_call | solution.py:712
  129.2 13.5 %backward_blocks.1 = (bf16[2,32,128,256]{3,2,1,0:T(8,128)(2,1)}, f32[256,512]{1,0:T(8,128)}, bf16[1,128,512]{2,1,0:T(8,128)(2,1)}, f32[8,128]{1,0:T(8,128)}) custom-call(s32[1,1,192]{2,1,0:T(1,128)} %source.3, s32[1,1,192]{2,1,0:T(1,128)} %target.3, s32[1,1,192]{2,1,0:T(1,128)} %relation.3, s32[1,1]{1,0:T(1,128)S(6)} %copy.21.live, ...), custom_call_target="tpu_custom_call" | custom-call | tf_op jit(solution)/shard_map/backward_blocks/pallas_call | solution.py:458
  142.7 48.8 %give_back.1 = (f32[1,128,512]{2,1,0:T(8,128)}, bf16[4,16,16,128]{3,2,1,0:T(8,128)(2,1)}, bf16[4,4,16,16,128]{4,3,2,1,0:T(8,128)(2,1)}) custom-call(bf16[2,8,4,128,256]{4,3,2,1,0:T(8,128)(2,1)} %bitcast.8, f32[256,512]{1,0:T(8,128)} %get-tuple-element.39.rel_part, bf16[4,128,512]{2,1,0:T(8,128)(2,1)} %get-tuple-element.40.agg_all, ...), custom_call_target="tpu_custom_call" | custom-call | tf_op jit(solution)/shard_map/give_back/pallas_call | solution.py:898
  191.5 3.0 %finish.1 = (f32[1,128,512]{2,1,0:T(8,128)}, f32[225,512]{1,0:T(8,128)}, f32[512,512]{1,0:T(8,128)}, f32[512,512]{1,0:T(8,128)}) custom-call(f32[1,128,512]{2,1,0:T(8,128)} %get-tuple-element.43.node_in, bf16[4,16,16,128]{3,2,1,0:T(8,128)(2,1)} %get-tuple-element.44.summed, bf16[4,4,16,16,128]{4,3,2,1,0:T(8,128)(2,1)} %get-tuple-element.45.w_all), custom_call_target="tpu_custom_call" | custom-call | tf_op jit(solution)/shard_map/finish/pallas_call | solution.py:940

commit v5 on v4

--- a/solution.py
+++ b/solution.py
@@ -57,14 +57,6 @@
     for device in devices:
         pl.semaphore_signal(barrier, inc=1, device_id=device, device_id_type=MESH)
     pl.semaphore_wait(barrier, len(devices))
-
-
-def ring_devices(me):
-    found = [me.sibling()]
-    for axis in ("y", "x", "z"):
-        for d in (1, 2, 3):
-            found.append(me.peer(axis, (me.at(axis) + d) % 4))
-    return found
 
 
 class Wire:
@@ -498,15 +490,50 @@
                 out[:, 256 * col : 256 * col + 256] = total
 
 
+class GatherY:
+    def __init__(self, me, wire, ref, slot):
+        self.me, self.wire, self.ref, self.slot = me, wire, ref, slot
+        self.near = (me.peer("y", (me.g + 1) % 4), me.peer("y", (me.g + 3) % 4))
+        self.first = [self.put(0, 0, 0), self.put(0, 1, 1)]
+        self.second = [self.put(0, 1, 0), self.put(0, 0, 1)]
+
+    def put(self, d, half, way):
+        place = self.ref.at[self.slot(d), pl.ds(64 * half, 64)]
+        return self.wire.put(place, place, self.near[way])
+
+    def neighbours(self):
+        self.first[0].wait_recv()
+        far = [self.put(1, 0, 0)]
+        self.first[1].wait_recv()
+        far.append(self.put(3, 1, 1))
+        for copy in self.second:
+            copy.wait_recv()
+        self.far = far
+
+    def opposite(self):
+        for copy in self.far:
+            copy.wait_recv()
+
+
 def middle_kernel(
     partial_low, partial, self_part, w_in, query_part, query_head, true_tail, allowed,
     h_out, loss, agg_all, pre_all, agg_tiles,
     share_recv, act, column, head_send, head_recv, queries, q_hi, q_lo, scores, stats,
-    grad_send, grad_recv, summed, g_hi, g_lo, rows, core_send, core_recv, y_send, y_recv,
+    h_sq, grad_send, grad_recv, summed, g_hi, g_lo, rows, core_send, core_recv, y_send, y_recv,
     send_sem, recv_sem,
 ):
     me = Place()
-    enter(ring_devices(me))
+    plane = []
+    for dx, dz in sorted(
+        [(i, j) for i in range(4) for j in range(4) if i or j],
+        key=lambda p: -(min(p[0], 4 - p[0]) + min(p[1], 4 - p[1])),
+    ):
+        plane.append(
+            me.dev(me.g, ((me.x + dx) % 4) * 8 + ((me.z + dz) % 4) * 2 + me.k)
+        )
+    enter(
+        [me.sibling()] + [me.peer("y", (me.g + d) % 4) for d in (1, 2, 3)] + plane
+    )
     wire = Wire(send_sem, recv_sem)
     count = true_tail.shape[1]
     scale = 512 ** (-0.5)
@@ -535,16 +562,19 @@
     h = activated.astype(BF)
     own_chunk = me.k * 4 + me.g
     column[own_chunk] = h
-    from_y = to_y(column, own_chunk)
+    gather_h = GatherY(me, wire, column, lambda d: me.k * 4 + (me.g + 4 - d) % 4)
     from_sibling = [wire.put(column.at[own_chunk], column.at[own_chunk], me.sibling())]
     h_out[0] = h
     act[...] = activated
     agg_all[me.g] = agg
-    agg_copies = to_y(agg_all, me.g)
+    gather_h.neighbours()
     for d in (1, 3, 2):
-        from_y[d].wait_recv()
+        if d == 2:
+            gather_h.opposite()
         chunk = me.k * 4 + (me.g + 4 - d) % 4
         from_sibling.append(wire.put(column.at[chunk], column.at[chunk], me.sibling()))
+
+    agg_copies = to_y(agg_all, me.g)
 
     head_row = jnp.broadcast_to(query_head[:, lanes] - base, (128, 128))
     head_col = head_row.astype(F32).T
@@ -558,7 +588,13 @@
         part = part + dot(pick, column[j])
     for col in range(2):
         head_send[0, col] = part[:, 256 * col : 256 * col + 256].astype(BF)
-    exchange_sum(me, wire, head_send, head_recv, summed)
+
+    def squares():
+        for j in range(8):
+            h32 = column[j].astype(F32)
+            h_sq[j] = jnp.broadcast_to(jnp.sum(h32 * h32, axis=1, keepdims=True), (128, 128))
+
+    exchange_sum(me, wire, head_send, head_recv, summed, squares)
 
     q = summed[...] + query_part[...]
     queries[...] = q
@@ -580,10 +616,8 @@
     masks = [jnp.broadcast_to(allowed_row(j), (128, 128)) > 0.5 for j in range(8)]
     tops, truths = [], []
     for j in range(8):
-        h32 = column[j].astype(F32)
-        h_sq = jnp.sum(h32 * h32, axis=1, keepdims=True)
         cross = dot(column[j], q_hi[...], NT) + dot(column[j], q_lo[...], NT)
-        score = -scale * (q_sq + h_sq - 2.0 * cross)
+        score = -scale * (q_sq + h_sq[j] - 2.0 * cross)
         scores[j] = score
         tops.append(jnp.max(jnp.where(masks[j], score, NEG_FILL), axis=0, keepdims=True))
         truths.append(
@@ -597,29 +631,21 @@
         weight = weight + jnp.sum(
             jnp.exp(jnp.where(masks[j], scores[j] - top, NEG_FILL)), axis=0, keepdims=True
         )
-    stats[0, 0, 0:1, :] = top
-    stats[0, 0, 1:2, :] = weight
-    stats[0, 0, 2:3, :] = functools.reduce(lambda a, b: a + b, truths)
-
-    for level, axis in enumerate(("z", "x")):
-        copies = []
-        for d in (1, 3, 2):
-            other = (me.at(axis) + d) % 4
-            copies.append(wire.put(stats.at[level, 0], stats.at[level, d], me.peer(axis, other)))
-        for copy in copies:
-            copy.wait_recv()
-        members = [stats[level, m] for m in range(4)]
-        tops = [m[0:1, :] for m in members]
-        top = functools.reduce(jnp.maximum, tops)
-        weight = members[0][1:2, :] * jnp.exp(tops[0] - top)
-        truth = members[0][2:3, :]
-        for m in range(1, 4):
-            weight = weight + members[m][1:2, :] * jnp.exp(tops[m] - top)
-            truth = truth + members[m][2:3, :]
-        if level == 0:
-            stats[1, 0, 0:1, :] = top
-            stats[1, 0, 1:2, :] = weight
-            stats[1, 0, 2:3, :] = truth
+    stats[0, 0:1, :] = top
+    stats[0, 1:2, :] = weight
+    stats[0, 2:3, :] = functools.reduce(lambda a, b: a + b, truths)
+
+    copies = [wire.put(stats.at[0], stats.at[e + 1], plane[e]) for e in range(15)]
+    for copy in copies:
+        copy.wait_recv()
+    members = [stats[m] for m in range(16)]
+    tops = [m[0:1, :] for m in members]
+    top = functools.reduce(jnp.maximum, tops)
+    weight = jnp.zeros((1, 128), F32)
+    truth = jnp.zeros((1, 128), F32)
+    for m in range(16):
+        weight = weight + members[m][1:2, :] * jnp.exp(tops[m] - top)
+        truth = truth + members[m][2:3, :]
     log_norm = top + jnp.log(weight)
     loss[group] = log_norm - truth
     loss_copies = to_y(loss, group)
@@ -692,10 +718,12 @@
     activated = act[...]
     pre_grad = (((2.0 * scale) * total) * (1.0 - activated * activated)).astype(BF)
     pre_all[me.g] = pre_grad
-    pre_copies = to_y(pre_all, me.g)
+    gather_pre = GatherY(me, wire, pre_all, lambda d: (me.g + 4 - d) % 4)
     agg_tiles[me.g] = dot(pre_grad, w_in[...], NT).astype(BF)
+    gather_pre.neighbours()
     for d in (1, 3, 2):
-        pre_copies[d].wait_recv()
+        if d == 2:
+            gather_pre.opposite()
         other = (me.g + 4 - d) % 4
         agg_tiles[other] = dot(pre_all[other], w_in[...], NT).astype(BF)
     for d in (1, 3, 2):
@@ -707,7 +735,7 @@
 
 def middle(partial_low, partial, self_part, w_in, query_part, query_head, true_tail, allowed):
     depth = w_in.shape[0]
-    copies = 64
+    copies = 3 + 6 + 4 + 3 + 12 + 15 + 3 + 12 + 4 + 3 + 4 + 6
     tile_bf = jax.ShapeDtypeStruct((4, 128, depth), BF)
     return pl.pallas_call(
         middle_kernel,
@@ -731,7 +759,8 @@
             pltpu.VMEM((128, depth), BF),
             pltpu.VMEM((128, depth), BF),
             pltpu.VMEM((8, 128, 128), F32),
-            pltpu.VMEM((2, 4, 8, 128), F32),
+            pltpu.VMEM((16, 8, 128), F32),
+            pltpu.VMEM((8, 128, 128), F32),
             pltpu.VMEM((2, 2, 128, 256), BF),
             pltpu.VMEM((2, 2, 3, 128, 256), BF),
             pltpu.VMEM((128, depth), F32),
@@ -777,22 +806,25 @@
         next(steps, None)
 
     axes = ((0, "x"), (1, "z"))
-    order = (1, 3, 2, 0)
     own_slots = (me.zk, me.xk)
     moved = {}
 
-    def send_round(d):
+    rounds = ((1, 0, 128), (3, 0, 128), (2, 0, 128), (0, 0, 64), (0, 64, 64))
+
+    def send_round(at):
+        d, start, size = rounds[at]
+        part = pl.ds(start, size)
         for col, axis in axes:
             place = (me.at(axis) + d) % 4
             for e in range(1, 8):
                 slot = (own_slots[col] + e) % 8
-                moved[d, col, e] = wire.put(
-                    tiles.at[col, slot, place],
-                    arrived.at[col, own_slots[col], place],
+                moved[at, col, e] = wire.put(
+                    tiles.at[col, slot, place, part],
+                    arrived.at[col, own_slots[col], place, part],
                     devices[7 * col + e - 1],
                 )
 
-    send_round(order[0])
+    send_round(0)
     local = []
     for col in range(2):
         copy = pltpu.make_async_copy(
@@ -816,7 +848,7 @@
                 .astype(BF)
             )
     advance()
-    send_round(order[1])
+    send_round(1)
     self_grad[...] = dot(pre_all[me.g], w_self[...], NT)
     advance()
     for copy in local:
@@ -825,8 +857,10 @@
     second = []
 
     def combine(d, col):
-        for copy in over_y[d, col]:
-            copy.wait_recv()
+        for at in range(len(rounds)):
+            if rounds[at][0] == d:
+                for copy in over_y[at, col]:
+                    copy.wait_recv()
         total = shipped[col, d, me.g].astype(F32)
         for m in range(3):
             total = total + y_recv[col, d, m].astype(F32)
@@ -843,34 +877,37 @@
                 )
             )
 
-    for at, d in enumerate(order):
+    for at, (d, start, size) in enumerate(rounds):
         for col, axis in axes:
             place = (me.at(axis) + d) % 4
             owner = place * 8 + me.zk if col == 0 else me.x * 8 + place * 2 + me.k
             for e in range(1, 8):
-                moved[d, col, e].wait_recv()
+                moved[at, col, e].wait_recv()
             index = [requests[8 * col + m, 0, owner] for m in range(8)]
-            for part in range(4):
-                rows = pl.ds(part * 32, 32)
+            for part in range(size // 32):
+                rows = pl.ds(start + part * 32, 32)
                 values = [arrived[col, m, place, rows, :].astype(F32) for m in range(8)]
                 for s in range(4):
                     total = jnp.zeros((32, 256), F32)
                     for m in range(8):
                         total = total + jnp.where(index[m] == s, values[m], 0.0)
                     shipped[col, d, s, rows, :] = total.astype(BF)
-            over_y[d, col] = []
+            over_y[at, col] = []
+            rows = pl.ds(start, size)
             for e in (1, 3, 2):
                 s = (me.g + e) % 4
-                over_y[d, col].append(
+                over_y[at, col].append(
                     wire.put(
-                        shipped.at[col, d, s], y_recv.at[col, d, e - 1], me.peer("y", s)
+                        shipped.at[col, d, s, rows],
+                        y_recv.at[col, d, e - 1, rows],
+                        me.peer("y", s),
                     )
                 )
         advance()
-        if at + 2 < 4:
-            send_round(order[at + 2])
-        if at:
-            send_combined(order[at - 1])
+        if at + 2 < len(rounds):
+            send_round(at + 2)
+        if at and rounds[at - 1][0]:
+            send_combined(rounds[at - 1][0])
     advance()
     pair = pl.ds(2 * me.k, 2)
     last = [
@@ -894,7 +931,7 @@
 def give_back(tiles, rel_part, agg_all, pre_all, node_tiles, w_self, requests):
     depth = w_self.shape[0]
     ar = AllReduce.scratch(16, STAGES_CAND, 32)
-    copies = 56 + 24 + 6 + (1 + 12 + 6 + 24) + 2
+    copies = 70 + 30 + 6 + (1 + 12 + 6 + 24) + 2
     return pl.pallas_call(
         functools.partial(return_kernel, len(ar)),
         name="give_back",

time: 195 us -> 191 us (0.979)
  Pallas kernels: 193 us -> 189 us
    pallas_call x1, Pallas kernels: 70.8 us -> 67.4 us  [middle(): pl.pallas_call(middle_kernel, name='middle', out_shape=(jax.ShapeDtypeStr...]
where the time goes in v5:
time: 191 us
  Pallas kernels  189 us (99%)
    pallas_call x1, Pallas kernels, middle(): pl.pallas_call(middle_kernel, name='middle', out_shape=(jax.ShapeDtypeStr...  67.4 us
    pallas_call x1, Pallas kernels, give_back(): pl.pallas_call(functools.partial(return_kernel, len(ar)), name='give_back...  48.4 us
    pallas_call x1, Pallas kernels, fetch(): pl.pallas_call(fetch_kernel, name='fetch', out_shape=(jax.ShapeDtypeStruc...  43.7 us
    pallas_call x1, Pallas kernels, backward(): pl.pallas_call(backward_kernel, name='backward_blocks', grid=(blocks // G...  13.5 us
    pallas_call x1, Pallas kernels, forward(): pl.pallas_call(forward_kernel, name='forward_blocks', grid=(blocks // GRO...  13.5 us

profile of v5, /device:TPU:1, one launch (start us, length us, event | category | flops | bytes accessed | tf_op | source)
XLA Modules:
  0.0 190.8 jit_solution(1439047837890766908)
XLA Ops:
  1.3 43.7 %fetch.1 = (bf16[2,8,4,128,256]{4,3,2,1,0:T(8,128)(2,1)}, s32[16,1,128]{2,1,0:T(1,128)}, f32[128,512]{1,0:T(8,128)}) custom-call(bf16[4,128,512]{2,1,0:T(8,128)(2,1)} %bitcast.10, s32[1,32]{1,0:T(1,128)} %bitcast.15, bf16[512,512]{1,0:T(8,128)(2,1)} %w_self.3), custom_call_target="tpu_custom_call" | custom-call | tf_op jit(solution)/shard_map/fetch/pallas_call | solution.py:304
  45.0 13.5 %forward_blocks.1 = (f32[4,128,512]{2,1,0:T(8,128)}, bf16[4,128,512]{2,1,0:T(8,128)(2,1)}, f32[128,512]{1,0:T(8,128)}) custom-call(s32[1,1,192]{2,1,0:T(1,128)} %source.3, s32[1,1,192]{2,1,0:T(1,128)} %target.3, s32[1,1,192]{2,1,0:T(1,128)} %relation.3, s32[1,1]{1,0:T(1,128)S(6)} %copy.21.live, bf16[1,1,192,128,128]{4,3,2,1,0:T(8,128)(2,1)} %values.3, ...), custom_call_target="tpu_custom_call" | custom-call | tf_op jit(solution)/shard_map/forward_blocks/pallas_call | solution.py:386
  58.5 67.4 %middle.1 = (bf16[1,128,512]{2,1,0:T(8,128)(2,1)}, f32[8,1,128]{2,1,0:T(1,128)}, bf16[4,128,512]{2,1,0:T(8,128)(2,1)}, bf16[4,128,512]{2,1,0:T(8,128)(2,1)}, bf16[4,128,512]{2,1,0:T(8,128)(2,1)}) custom-call(bf16[4,128,512]{2,1,0:T(8,128)(2,1)} %get-tuple-element.29.partial_low, f32[4,128,512]{2,1,0:T(8,128)} %get-tuple-element.30.partial, ...), custom_call_target="tpu_custom_call" | custom-call | tf_op jit(solution)/shard_map/middle/pallas_call | solution.py:740
  125.8 13.5 %backward_blocks.1 = (bf16[2,32,128,256]{3,2,1,0:T(8,128)(2,1)}, f32[256,512]{1,0:T(8,128)}, bf16[1,128,512]{2,1,0:T(8,128)(2,1)}, f32[8,128]{1,0:T(8,128)}) custom-call(s32[1,1,192]{2,1,0:T(1,128)} %source.3, s32[1,1,192]{2,1,0:T(1,128)} %target.3, s32[1,1,192]{2,1,0:T(1,128)} %relation.3, s32[1,1]{1,0:T(1,128)S(6)} %copy.21.live, ...), custom_call_target="tpu_custom_call" | custom-call | tf_op jit(solution)/shard_map/backward_blocks/pallas_call | solution.py:450
  139.3 48.4 %give_back.1 = (f32[1,128,512]{2,1,0:T(8,128)}, bf16[4,16,16,128]{3,2,1,0:T(8,128)(2,1)}, bf16[4,4,16,16,128]{4,3,2,1,0:T(8,128)(2,1)}) custom-call(bf16[2,8,4,128,256]{4,3,2,1,0:T(8,128)(2,1)} %bitcast.8, f32[256,512]{1,0:T(8,128)} %get-tuple-element.39.rel_part, bf16[4,128,512]{2,1,0:T(8,128)(2,1)} %get-tuple-element.40.agg_all, ...), custom_call_target="tpu_custom_call" | custom-call | tf_op jit(solution)/shard_map/give_back/pallas_call | solution.py:935
  187.7 3.0 %finish.1 = (f32[1,128,512]{2,1,0:T(8,128)}, f32[225,512]{1,0:T(8,128)}, f32[512,512]{1,0:T(8,128)}, f32[512,512]{1,0:T(8,128)}) custom-call(f32[1,128,512]{2,1,0:T(8,128)} %get-tuple-element.43.node_in, bf16[4,16,16,128]{3,2,1,0:T(8,128)(2,1)} %get-tuple-element.44.summed, bf16[4,4,16,16,128]{4,3,2,1,0:T(8,128)(2,1)} %get-tuple-element.45.w_all), custom_call_target="tpu_custom_call" | custom-call | tf_op jit(solution)/shard_map/finish/pallas_call | solution.py:977

commit v6 on v5

--- a/solution.py
+++ b/solution.py
@@ -17,7 +17,7 @@
 VMEM_SPEC = pl.BlockSpec(memory_space=pltpu.VMEM)
 SMEM_SPEC = pl.BlockSpec(memory_space=pltpu.SMEM)
 ANY_SPEC = pl.BlockSpec(memory_space=pl.ANY)
-LIMIT = 60 * 1024 * 1024
+MIB = 1024 * 1024
 STAGES_CAND = (("z", "x"), ("x", "z"))
 
 
@@ -304,6 +304,7 @@
     return pl.pallas_call(
         fetch_kernel,
         name="fetch",
+        cost_estimate=pl.CostEstimate(flops=67108864, bytes_accessed=100000000, transcendentals=0),
         out_shape=(
             jax.ShapeDtypeStruct((2, 8, 4, 128, 256), BF),
             jax.ShapeDtypeStruct((16, 1, 128), jnp.int32),
@@ -321,7 +322,7 @@
             *[pltpu.VMEM((4, 128, 256), BF)] * 6,
         ],
         compiler_params=pltpu.CompilerParams(
-            collective_id=0, has_side_effects=True, vmem_limit_bytes=LIMIT
+            collective_id=0, has_side_effects=True, vmem_limit_bytes=16 * MIB
         ),
     )(node_tiles, wanted, w_self)
 
@@ -386,6 +387,7 @@
     return pl.pallas_call(
         forward_kernel,
         name="forward_blocks",
+        cost_estimate=pl.CostEstimate(flops=3221225472, bytes_accessed=30000000, transcendentals=0),
         grid=(blocks // GROUP,),
         out_shape=(
             jax.ShapeDtypeStruct((4, 128, depth), F32),
@@ -394,7 +396,7 @@
         ),
         in_specs=adjacency_specs(blocks) + [VMEM_SPEC] * 2 + [SMEM_SPEC, VMEM_SPEC],
         out_specs=(VMEM_SPEC,) * 3,
-        compiler_params=pltpu.CompilerParams(vmem_limit_bytes=LIMIT),
+        compiler_params=pltpu.CompilerParams(vmem_limit_bytes=16 * MIB),
     )(
         adj_source, adj_target, adj_relation, live_blocks, adj_values,
         mirrors.reshape(2, 32, 128, 256), rel_emb, query_rel, rel_score,
@@ -450,6 +452,7 @@
     return pl.pallas_call(
         backward_kernel,
         name="backward_blocks",
+        cost_estimate=pl.CostEstimate(flops=3221225472, bytes_accessed=30000000, transcendentals=0),
         grid=(blocks // GROUP,),
         out_shape=(
             jax.ShapeDtypeStruct((2, 32, 128, 256), BF),
@@ -460,7 +463,7 @@
         in_specs=adjacency_specs(blocks) + [VMEM_SPEC] * 3,
         out_specs=(VMEM_SPEC,) * 4,
         scratch_shapes=[pltpu.VMEM((2, 32, 128, 256), F32)],
-        compiler_params=pltpu.CompilerParams(vmem_limit_bytes=LIMIT),
+        compiler_params=pltpu.CompilerParams(vmem_limit_bytes=24 * MIB),
     )(adj_source, adj_target, adj_relation, live_blocks, adj_values, agg_tiles, h, loss)
 
 
@@ -740,6 +743,7 @@
     return pl.pallas_call(
         middle_kernel,
         name="middle",
+        cost_estimate=pl.CostEstimate(flops=2000000000, bytes_accessed=150000000, transcendentals=0),
         out_shape=(
             jax.ShapeDtypeStruct((1, 128, depth), BF),
             jax.ShapeDtypeStruct((8, 1, 128), F32),
@@ -775,7 +779,7 @@
             pltpu.SemaphoreType.DMA((copies,)),
         ],
         compiler_params=pltpu.CompilerParams(
-            collective_id=1, has_side_effects=True, vmem_limit_bytes=LIMIT
+            collective_id=1, has_side_effects=True, vmem_limit_bytes=22 * MIB
         ),
     )(partial_low, partial, self_part, w_in, query_part, query_head, true_tail, allowed)
 
@@ -935,6 +939,7 @@
     return pl.pallas_call(
         functools.partial(return_kernel, len(ar)),
         name="give_back",
+        cost_estimate=pl.CostEstimate(flops=1000000000, bytes_accessed=120000000, transcendentals=0),
         out_shape=(
             jax.ShapeDtypeStruct((1, 128, depth), F32),
             jax.ShapeDtypeStruct((4, 16, 16, 128), BF),
@@ -955,36 +960,42 @@
             pltpu.SemaphoreType.DMA((2,)),
         ],
         compiler_params=pltpu.CompilerParams(
-            collective_id=2, has_side_effects=True, vmem_limit_bytes=LIMIT
+            collective_id=2, has_side_effects=True, vmem_limit_bytes=20 * MIB
         ),
     )(tiles, rel_part, agg_all, pre_all, node_tiles, w_self, requests)
 
 
 def finish_kernel(node_in, summed, w_all, node_grad, rel_grad, w_in_grad, w_self_grad):
     node_grad[...] = node_in[...]
-    for j in range(4):
-        cols = slice(128 * j, 128 * j + 128)
-        whole = summed[j].astype(F32).reshape(256, 128)
-        rel_grad[:, cols] = whole[: rel_grad.shape[0]]
-        for q in range(2):
-            rows = slice(256 * q, 256 * q + 256)
-            for at, target in ((q, w_in_grad), (2 + q, w_self_grad)):
-                target[rows, cols] = w_all[j, at].astype(F32).reshape(256, 128)
+    whole = summed[0].astype(F32).reshape(256, 128)
+    rel_grad[...] = whole[: rel_grad.shape[0]]
+    for q in range(2):
+        rows = slice(256 * q, 256 * q + 256)
+        for at, target in ((q, w_in_grad), (2 + q, w_self_grad)):
+            target[rows, :] = w_all[0, at].astype(F32).reshape(256, 128)
 
 
 def finish(node_grad, summed, w_all, relations):
     depth = node_grad.shape[2]
+    tile = pl.BlockSpec((1, 128, 128), lambda j: (0, 0, j))
+    whole = pl.BlockSpec((depth, 128), lambda j: (0, j))
     return pl.pallas_call(
         finish_kernel,
         name="finish",
+        grid=(4,),
         out_shape=(
             jax.ShapeDtypeStruct(node_grad.shape, F32),
             jax.ShapeDtypeStruct((relations, depth), F32),
             jax.ShapeDtypeStruct((depth, depth), F32),
             jax.ShapeDtypeStruct((depth, depth), F32),
         ),
-        in_specs=[VMEM_SPEC] * 3,
-        out_specs=(VMEM_SPEC,) * 4,
+        in_specs=[
+            tile,
+            pl.BlockSpec((1, 16, 16, 128), lambda j: (j, 0, 0, 0)),
+            pl.BlockSpec((1, 4, 16, 16, 128), lambda j: (j, 0, 0, 0, 0)),
+        ],
+        out_specs=(tile, pl.BlockSpec((relations, 128), lambda j: (0, j)), whole, whole),
+        compiler_params=pltpu.CompilerParams(vmem_limit_bytes=8 * MIB),
     )(node_grad, summed, w_all)
 
 
@@ -1009,8 +1020,9 @@
     node_tiles = node_emb.reshape(4, 128, -1)
     mirrors, requests, self_part = fetch(node_tiles, wanted, w_self)
     partial, partial_low, query_part = forward(
-        adj_source, adj_target, adj_relation, live_blocks, adj_values, mirrors, rel_emb,
-        query_rel, rel_score,
+        adj_source, adj_target, adj_relation, live_blocks,
+        pltpu.with_memory_space_constraint(adj_values, pltpu.HBM),
+        mirrors, rel_emb, query_rel, rel_score,
     )
     h, loss, agg_all, pre_all, agg_tiles = middle(
         partial_low,

time: 191 us -> 185 us (0.969)
  Pallas kernels: 189 us -> 175 us
  local copies, waits for them, and re-layouts: 0 us -> 8.34 us
    pallas_call x5, Pallas kernels: 141 us -> 128 us  [the longest x1 64 us: middle(): pl.pallas_call(middle_kernel, name='middle', cost_estimate=pl.CostEstimat...]
    unnamed x0 -> x40, local copies, waits for them, and re-layouts: none -> 8.34 us
    pallas_call x1, Pallas kernels: 48.4 us -> 46.2 us  [give_back(): pl.pallas_call(functools.partial(return_kernel, len(ar)), name='give_back...]
where the time goes in v6:
time: 185 us
  Pallas kernels  175 us (95%)
  local copies, waits for them, and re-layouts  8.34 us (5%)
    pallas_call x1, Pallas kernels, middle(): pl.pallas_call(middle_kernel, name='middle', cost_estimate=pl.CostEstimat...  64 us
    pallas_call x1, Pallas kernels, give_back(): pl.pallas_call(functools.partial(return_kernel, len(ar)), name='give_back...  46.2 us
    pallas_call x1, Pallas kernels, fetch(): pl.pallas_call(fetch_kernel, name='fetch', cost_estimate=pl.CostEstimate(...  40.4 us
    pallas_call x1, Pallas kernels, forward(): pl.pallas_call(forward_kernel, name='forward_blocks', cost_estimate=pl.Co...  11.1 us
    pallas_call x1, Pallas kernels, backward(): pl.pallas_call(backward_kernel, name='backward_blocks', cost_estimate=pl....  10.9 us
    unnamed x40, local copies, waits for them, and re-layouts  8.34 us

profile of v6, /device:TPU:1, one launch (start us, length us, event | category | flops | bytes accessed | tf_op | source)
XLA Modules:
  0.0 184.5 jit_solution(6184418629509429390)
XLA Ops:
  1.3 0.0 copy-start
  1.3 1.0 copy-done
  2.3 0.0 copy-start.2
  2.3 1.0 copy-done.2
  3.4 0.0 copy-start.13
  3.4 0.7 copy-done.13
  4.0 40.4 %fetch.1 = (bf16[2,8,4,128,256]{4,3,2,1,0:T(8,128)(2,1)S(1)}, s32[16,1,128]{2,1,0:T(1,128)S(1)}, f32[128,512]{1,0:T(8,128)S(1)}) custom-call(bf16[4,128,512]{2,1,0:T(8,128)(2,1)S(1)} %bitcast.12, s32[1,32]{1,0:T(1,128)S(1)} %bitcast.14, bf16[512,512]{1,0:T(8,128)(2,1)S(1)} %copy-done.2), custom_call_target="tpu_custom_call" | custom-call | flops 67108864 | bytes 100000000 | tf_op jit(solution)/shard_map/fetch/pallas_call | solution.py:304
  44.4 0.0 slice-start
  44.5 0.0 copy-start.4
  44.5 1.6 copy-done.4
  46.1 0.0 copy-start.5
  46.1 1.2 copy-done.5
  47.3 0.0 copy-start.6
  47.3 0.7 copy-done.6
  48.0 0.0 copy-start.7
  48.0 0.7 copy-done.7
  48.7 0.0 copy-start.9
  48.7 0.7 copy-done.9
  49.3 0.0 copy-start.11
  49.3 0.7 copy-done.11
  50.0 0.0 copy-start.14
  50.0 0.0 copy-start.15
  50.0 0.0 copy-start.16
  50.0 0.0 copy-start.17
  50.0 0.0 slice-start.1
  50.0 11.1 %forward_blocks.1 = (f32[4,128,512]{2,1,0:T(8,128)S(1)}, bf16[4,128,512]{2,1,0:T(8,128)(2,1)S(1)}, f32[128,512]{1,0:T(8,128)S(1)}) custom-call(s32[1,1,192]{2,1,0:T(1,128)S(1)} %copy-done.7, s32[1,1,192]{2,1,0:T(1,128)S(1)} %copy-done.9, s32[1,1,192]{2,1,0:T(1,128)S(1)} %copy-done.11, s32[1,1]{1,0:T(1,128)S(6)} %copy.21.live, ...), custom_call_target="tpu_custom_call" | custom-call | flops 3221225472 | bytes 30000000 | tf_op jit(solution)/shard_map/forward_blocks/pallas_call | solution.py:387
  61.1 0.0 copy-start.8
  61.2 0.0 copy-start.10
  61.2 0.0 copy-start.12
  61.2 0.0 copy-done.14
  61.2 0.0 copy-done.15
  61.2 0.0 copy-done.16
  61.2 0.0 copy-done.17
  61.2 64.0 %middle.1 = (bf16[1,128,512]{2,1,0:T(8,128)(2,1)S(1)}, f32[8,1,128]{2,1,0:T(1,128)S(1)}, bf16[4,128,512]{2,1,0:T(8,128)(2,1)S(1)}, bf16[4,128,512]{2,1,0:T(8,128)(2,1)S(1)}, bf16[4,128,512]{2,1,0:T(8,128)(2,1)S(1)}) custom-call(bf16[4,128,512]{2,1,0:T(8,128)(2,1)S(1)} %get-tuple-element.29.partial_low, f32[4,128,512]{2,1,0:T(8,128)S(1)} %get-tuple-element.30.partial, ...), custom_call_target="tpu_custom_call" | custom-call | flops 2000000000 | bytes 150000000 | tf_op jit(solution)/shard_map/middle/pallas_call | solution.py:743
  125.2 0.0 slice-done
  125.2 0.0 slice-done.1
  125.3 0.0 copy-done.8
  125.3 0.0 copy-done.10
  125.3 0.0 copy-done.12
  125.3 0.0 copy-start.1
  125.3 0.0 copy-start.3
  125.3 10.9 %backward_blocks.1 = (bf16[2,32,128,256]{3,2,1,0:T(8,128)(2,1)S(1)}, f32[256,512]{1,0:T(8,128)S(1)}, bf16[1,128,512]{2,1,0:T(8,128)(2,1)}, f32[8,128]{1,0:T(8,128)}) custom-call(s32[1,1,192]{2,1,0:T(1,128)S(1)} %copy-done.8, s32[1,1,192]{2,1,0:T(1,128)S(1)} %copy-done.10, s32[1,1,192]{2,1,0:T(1,128)S(1)} %copy-done.12, s32[1,1]{1,0:T(1,128)S(6)} %copy.21.live, ...), custom_call_target="tpu_custom_call" | custom-call | flops 3221225472 | bytes 30000000 | tf_op jit(solution)/shard_map/backward_blocks/pallas_call | solution.py:452
  136.2 0.0 copy-done.1
  136.2 0.0 copy-done.3
  136.2 46.2 %give_back.1 = (f32[1,128,512]{2,1,0:T(8,128)S(1)}, bf16[4,16,16,128]{3,2,1,0:T(8,128)(2,1)S(1)}, bf16[4,4,16,16,128]{4,3,2,1,0:T(8,128)(2,1)S(1)}) custom-call(bf16[2,8,4,128,256]{4,3,2,1,0:T(8,128)(2,1)S(1)} %bitcast.10, f32[256,512]{1,0:T(8,128)S(1)} %get-tuple-element.39.rel_part, bf16[4,128,512]{2,1,0:T(8,128)(2,1)S(1)} %get-tuple-element.40.agg_all, ...), custom_call_target="tpu_custom_call" | custom-call | flops 1000000000 | bytes 120000000 | tf_op jit(solution)/shard_map/give_back/pallas_call | solution.py:939
  182.5 2.1 %finish.1 = (f32[1,128,512]{2,1,0:T(8,128)}, f32[225,512]{1,0:T(8,128)}, f32[512,512]{1,0:T(8,128)}, f32[512,512]{1,0:T(8,128)}) custom-call(f32[1,128,512]{2,1,0:T(8,128)S(1)} %get-tuple-element.43.node_in, bf16[4,16,16,128]{3,2,1,0:T(8,128)(2,1)S(1)} %get-tuple-element.44.summed, bf16[4,4,16,16,128]{4,3,2,1,0:T(8,128)(2,1)S(1)} %get-tuple-element.45.w_all), custom_call_target="tpu_custom_call" | custom-call | tf_op jit(solution)/shard_map/finish/pallas_call | solution.py:982
  (1 shorter events, 0.0 us)
Async XLA Ops:
  1.3 1.0 copy-start
  2.3 1.0 copy-start.2
  3.4 0.7 copy-start.13
  44.4 80.8 %slice-start = ((s8[6291456]{0:T(1024)(128)(4,1)}), s8[4194304]{0:T(1024)(128)(4,1)S(1)}, s32[]{:S(2)}) async-start(s8[6291456]{0:T(1024)(128)(4,1)} %bitcast.8), calls=%async_computation | async-start | bytes 8388608
  44.5 1.7 copy-start.4
  46.1 1.2 copy-start.5
  47.3 0.7 copy-start.6
  48.0 0.7 copy-start.7
  48.7 0.7 copy-start.9
  49.3 0.7 copy-start.11
  50.0 11.2 %copy-start.14 = (bf16[512,512]{1,0:T(8,128)(2,1)S(1)}, bf16[512,512]{1,0:T(8,128)(2,1)}, u32[]{:S(2)}) copy-start(bf16[512,512]{1,0:T(8,128)(2,1)} %w_in.1) | copy-start | bytes 1572868
  50.0 11.2 %copy-start.15 = (s32[1024,8]{0,1:T(8,128)S(1)}, s32[1024,8]{0,1:T(8,128)}, u32[]{:S(2)}) copy-start(s32[1024,8]{0,1:T(8,128)} %param.28) | copy-start | bytes 98308
  50.0 11.2 %copy-start.16 = (s32[1024]{0:T(1024)S(1)}, s32[1024]{0:T(1024)}, u32[]{:S(2)}) copy-start(s32[1024]{0:T(1024)} %param.26) | copy-start | bytes 12292
  50.0 11.2 %copy-start.17 = (s32[1024]{0:T(1024)S(1)}, s32[1024]{0:T(1024)}, u32[]{:S(2)}) copy-start(s32[1024]{0:T(1024)} %param.29) | copy-start | bytes 12292
  50.0 75.2 %slice-start.1 = ((s8[6291456]{0:T(1024)(128)(4,1)}), s8[2097152]{0:T(1024)(128)(4,1)S(1)}, s32[]{:S(2)}) async-start(s8[6291456]{0:T(1024)(128)(4,1)} %bitcast.8), calls=%async_computation.1 | async-start | bytes 4194304
  61.1 64.1 %copy-start.8 = (s32[1,1,192]{2,1,0:T(1,128)S(1)}, s32[1,1,192]{2,1,0:T(1,128)}, u32[]{:S(2)}) copy-start(s32[1,1,192]{2,1,0:T(1,128)} %source.3) | copy-start | bytes 2308
  61.2 64.1 %copy-start.10 = (s32[1,1,192]{2,1,0:T(1,128)S(1)}, s32[1,1,192]{2,1,0:T(1,128)}, u32[]{:S(2)}) copy-start(s32[1,1,192]{2,1,0:T(1,128)} %target.3) | copy-start | bytes 2308
  61.2 64.1 %copy-start.12 = (s32[1,1,192]{2,1,0:T(1,128)S(1)}, s32[1,1,192]{2,1,0:T(1,128)}, u32[]{:S(2)}) copy-start(s32[1,1,192]{2,1,0:T(1,128)} %relation.3) | copy-start | bytes 2308
  125.3 10.9 %copy-start.1 = (bf16[1,512,512]{2,1,0:T(8,128)(2,1)S(1)}, bf16[1,512,512]{2,1,0:T(8,128)(2,1)}, u32[]{:S(2)}) copy-start(bf16[1,512,512]{2,1,0:T(8,128)(2,1)} %param.15) | copy-start | bytes 1572868
  125.3 10.9 %copy-start.3 = (bf16[512,512]{1,0:T(8,128)(2,1)S(1)}, bf16[512,512]{1,0:T(8,128)(2,1)}, u32[]{:S(2)}) copy-start(bf16[512,512]{1,0:T(8,128)(2,1)} %w_self.3) | copy-start | bytes 1572868

commit v7 on v6

--- a/solution.py
+++ b/solution.py
@@ -999,6 +999,10 @@
     )(node_grad, summed, w_all)
 
 
+def stay(array):
+    return pltpu.with_memory_space_constraint(array, pltpu.HBM)
+
+
 def body(
     node_emb,
     rel_emb,
@@ -1018,11 +1022,10 @@
 ):
     wanted = mirror_blocks.reshape(1, 32)
     node_tiles = node_emb.reshape(4, 128, -1)
-    mirrors, requests, self_part = fetch(node_tiles, wanted, w_self)
+    mirrors, requests, self_part = fetch(stay(node_tiles), stay(wanted), stay(w_self))
     partial, partial_low, query_part = forward(
-        adj_source, adj_target, adj_relation, live_blocks,
-        pltpu.with_memory_space_constraint(adj_values, pltpu.HBM),
-        mirrors, rel_emb, query_rel, rel_score,
+        stay(adj_source), stay(adj_target), stay(adj_relation), live_blocks, stay(adj_values),
+        mirrors, stay(rel_emb), stay(query_rel), stay(rel_score),
     )
     h, loss, agg_all, pre_all, agg_tiles = middle(
         partial_low,

time: 185 us -> 178 us (0.962)
  local copies, waits for them, and re-layouts: 8.34 us -> 0.07 us
    unnamed x40 -> x22, local copies, waits for them, and re-layouts: 8.34 us -> 0.07 us
where the time goes in v7:
time: 178 us
  Pallas kernels  176 us (99%)
    pallas_call x1, Pallas kernels, middle(): pl.pallas_call(middle_kernel, name='middle', cost_estimate=pl.CostEstimat...  65.6 us
    pallas_call x1, Pallas kernels, give_back(): pl.pallas_call(functools.partial(return_kernel, len(ar)), name='give_back...  46.7 us
    pallas_call x1, Pallas kernels, fetch(): pl.pallas_call(fetch_kernel, name='fetch', cost_estimate=pl.CostEstimate(...  41.7 us
    pallas_call x1, Pallas kernels, forward(): pl.pallas_call(forward_kernel, name='forward_blocks', cost_estimate=pl.Co...  10.1 us
    pallas_call x1, Pallas kernels, backward(): pl.pallas_call(backward_kernel, name='backward_blocks', cost_estimate=pl....  9.87 us

profile of v7, /device:TPU:1, one launch (start us, length us, event | category | flops | bytes accessed | tf_op | source)
XLA Modules:
  0.0 177.6 jit_solution(13532886949993100803)
XLA Ops:
  1.3 41.7 %fetch.1 = (bf16[2,8,4,128,256]{4,3,2,1,0:T(8,128)(2,1)S(1)}, s32[16,1,128]{2,1,0:T(1,128)S(1)}, f32[128,512]{1,0:T(8,128)S(1)}) custom-call(bf16[4,128,512]{2,1,0:T(8,128)(2,1)} %bitcast.12, s32[1,32]{1,0:T(1,128)} %bitcast.17, bf16[512,512]{1,0:T(8,128)(2,1)} %w_self.3), custom_call_target="tpu_custom_call" | custom-call | flops 67108864 | bytes 100000000 | tf_op jit(solution)/shard_map/fetch/pallas_call | solution.py:304
  43.0 0.0 slice-start
  43.0 0.0 copy-start.5
  43.0 0.0 copy-start.6
  43.0 0.0 copy-start.7
  43.0 0.0 copy-start.8
  43.0 0.0 slice-start.1
  43.1 10.1 %forward_blocks.1 = (f32[4,128,512]{2,1,0:T(8,128)S(1)}, bf16[4,128,512]{2,1,0:T(8,128)(2,1)S(1)}, f32[128,512]{1,0:T(8,128)S(1)}) custom-call(s32[1,1,192]{2,1,0:T(1,128)} %source.3, s32[1,1,192]{2,1,0:T(1,128)} %target.3, s32[1,1,192]{2,1,0:T(1,128)} %relation.3, s32[1,1]{1,0:T(1,128)S(6)} %copy.21.live, bf16[1,1,192,128,128]{4,3,2,1,0:T(8,128)(2,1)} %values.3, ...), custom_call_target="tpu_custom_call" | custom-call | flops 3221225472 | bytes 30000000 | tf_op jit(solution)/shard_map/forward_blocks/pallas_call | solution.py:387
  53.2 0.0 copy-start.2
  53.2 0.0 copy-start.3
  53.2 0.0 copy-start.4
  53.2 0.0 copy-done.5
  53.2 0.0 copy-done.6
  53.2 0.0 copy-done.7
  53.2 0.0 copy-done.8
  53.2 65.6 %middle.1 = (bf16[1,128,512]{2,1,0:T(8,128)(2,1)S(1)}, f32[8,1,128]{2,1,0:T(1,128)S(1)}, bf16[4,128,512]{2,1,0:T(8,128)(2,1)S(1)}, bf16[4,128,512]{2,1,0:T(8,128)(2,1)S(1)}, bf16[4,128,512]{2,1,0:T(8,128)(2,1)S(1)}) custom-call(bf16[4,128,512]{2,1,0:T(8,128)(2,1)S(1)} %get-tuple-element.29.partial_low, f32[4,128,512]{2,1,0:T(8,128)S(1)} %get-tuple-element.30.partial, ...), custom_call_target="tpu_custom_call" | custom-call | flops 2000000000 | bytes 150000000 | tf_op jit(solution)/shard_map/middle/pallas_call | solution.py:743
  118.9 0.0 slice-done
  118.9 0.0 slice-done.1
  118.9 0.0 copy-done.2
  118.9 0.0 copy-done.3
  118.9 0.0 copy-done.4
  118.9 0.0 copy-start
  118.9 0.0 copy-start.1
  118.9 9.9 %backward_blocks.1 = (bf16[2,32,128,256]{3,2,1,0:T(8,128)(2,1)S(1)}, f32[256,512]{1,0:T(8,128)S(1)}, bf16[1,128,512]{2,1,0:T(8,128)(2,1)}, f32[8,128]{1,0:T(8,128)}) custom-call(s32[1,1,192]{2,1,0:T(1,128)S(1)} %copy-done.2, s32[1,1,192]{2,1,0:T(1,128)S(1)} %copy-done.3, s32[1,1,192]{2,1,0:T(1,128)S(1)} %copy-done.4, s32[1,1]{1,0:T(1,128)S(6)} %copy.21.live, ...), custom_call_target="tpu_custom_call" | custom-call | flops 3221225472 | bytes 30000000 | tf_op jit(solution)/shard_map/backward_blocks/pallas_call | solution.py:452
  128.8 0.0 copy-done
  128.8 0.0 copy-done.1
  128.8 46.7 %give_back.1 = (f32[1,128,512]{2,1,0:T(8,128)S(1)}, bf16[4,16,16,128]{3,2,1,0:T(8,128)(2,1)S(1)}, bf16[4,4,16,16,128]{4,3,2,1,0:T(8,128)(2,1)S(1)}) custom-call(bf16[2,8,4,128,256]{4,3,2,1,0:T(8,128)(2,1)S(1)} %bitcast.10, f32[256,512]{1,0:T(8,128)S(1)} %get-tuple-element.39.rel_part, bf16[4,128,512]{2,1,0:T(8,128)(2,1)S(1)} %get-tuple-element.40.agg_all, ...), custom_call_target="tpu_custom_call" | custom-call | flops 1000000000 | bytes 120000000 | tf_op jit(solution)/shard_map/give_back/pallas_call | solution.py:939
  175.6 2.1 %finish.1 = (f32[1,128,512]{2,1,0:T(8,128)}, f32[225,512]{1,0:T(8,128)}, f32[512,512]{1,0:T(8,128)}, f32[512,512]{1,0:T(8,128)}) custom-call(f32[1,128,512]{2,1,0:T(8,128)S(1)} %get-tuple-element.43.node_in, bf16[4,16,16,128]{3,2,1,0:T(8,128)(2,1)S(1)} %get-tuple-element.44.summed, bf16[4,4,16,16,128]{4,3,2,1,0:T(8,128)(2,1)S(1)} %get-tuple-element.45.w_all), custom_call_target="tpu_custom_call" | custom-call | tf_op jit(solution)/shard_map/finish/pallas_call | solution.py:982
  (1 shorter events, 0.0 us)
Async XLA Ops:
  43.0 75.9 %slice-start = ((s8[6291456]{0:T(1024)(128)(4,1)}), s8[4194304]{0:T(1024)(128)(4,1)S(1)}, s32[]{:S(2)}) async-start(s8[6291456]{0:T(1024)(128)(4,1)} %bitcast.8), calls=%async_computation | async-start | bytes 8388608
  43.0 10.2 %copy-start.5 = (bf16[512,512]{1,0:T(8,128)(2,1)S(1)}, bf16[512,512]{1,0:T(8,128)(2,1)}, u32[]{:S(2)}) copy-start(bf16[512,512]{1,0:T(8,128)(2,1)} %w_in.1) | copy-start | bytes 1572868
  43.0 10.2 %copy-start.6 = (s32[1024,8]{0,1:T(8,128)S(1)}, s32[1024,8]{0,1:T(8,128)}, u32[]{:S(2)}) copy-start(s32[1024,8]{0,1:T(8,128)} %param.28) | copy-start | bytes 98308
  43.0 10.2 %copy-start.7 = (s32[1024]{0:T(1024)S(1)}, s32[1024]{0:T(1024)}, u32[]{:S(2)}) copy-start(s32[1024]{0:T(1024)} %param.26) | copy-start | bytes 12292
  43.0 10.2 %copy-start.8 = (s32[1024]{0:T(1024)S(1)}, s32[1024]{0:T(1024)}, u32[]{:S(2)}) copy-start(s32[1024]{0:T(1024)} %param.29) | copy-start | bytes 12292
  43.0 75.8 %slice-start.1 = ((s8[6291456]{0:T(1024)(128)(4,1)}), s8[2097152]{0:T(1024)(128)(4,1)S(1)}, s32[]{:S(2)}) async-start(s8[6291456]{0:T(1024)(128)(4,1)} %bitcast.8), calls=%async_computation.1 | async-start | bytes 4194304
  53.2 65.7 %copy-start.2 = (s32[1,1,192]{2,1,0:T(1,128)S(1)}, s32[1,1,192]{2,1,0:T(1,128)}, u32[]{:S(2)}) copy-start(s32[1,1,192]{2,1,0:T(1,128)} %source.3) | copy-start | bytes 2308
  53.2 65.7 %copy-start.3 = (s32[1,1,192]{2,1,0:T(1,128)S(1)}, s32[1,1,192]{2,1,0:T(1,128)}, u32[]{:S(2)}) copy-start(s32[1,1,192]{2,1,0:T(1,128)} %target.3) | copy-start | bytes 2308
  53.2 65.7 %copy-start.4 = (s32[1,1,192]{2,1,0:T(1,128)S(1)}, s32[1,1,192]{2,1,0:T(1,128)}, u32[]{:S(2)}) copy-start(s32[1,1,192]{2,1,0:T(1,128)} %relation.3) | copy-start | bytes 2308
  118.9 9.9 %copy-start = (bf16[1,512,512]{2,1,0:T(8,128)(2,1)S(1)}, bf16[1,512,512]{2,1,0:T(8,128)(2,1)}, u32[]{:S(2)}) copy-start(bf16[1,512,512]{2,1,0:T(8,128)(2,1)} %param.15) | copy-start | bytes 1572868
  118.9 9.9 %copy-start.1 = (bf16[512,512]{1,0:T(8,128)(2,1)S(1)}, bf16[512,512]{1,0:T(8,128)(2,1)}, u32[]{:S(2)}) copy-start(bf16[512,512]{1,0:T(8,128)(2,1)} %w_self.3) | copy-start | bytes 1572868
